TPU v7x, 768 devices: a whole 4x8x12 slice. The times are simulated.
768 devices in a mesh: member: 16 (over z_hi, x), space: 48 (over z_lo, y, core).
Axes of the slice: x: 4, y: 8, z: 12 (z_hi: 4, z_lo: 3; z = z_hi * 3 + z_lo), core: 2. Of those that a mesh axis runs over, the one named last changes fastest.
Arguments:
- perturb: float32 [16, 192, 96, 192], P('member', 'space'), may hold values from -8 to 8
- register: float32 [16, 192, 18432], P('member', 'space'), may hold values from -6 to 6
- ref_velocity: float32 [3, 192, 192], P(None, 'space', 'member'), may hold values from -6 to 6
Outputs:
- advanced_perturb: float32 [16, 192, 18432], P('member', 'space')
- advanced_register: float32 [16, 192, 18432], P('member', 'space')
- reference_step: float32 [3, 192, 192], P(None, 'member', 'space')
- gram: float32 [16, 16], P('member')
All inputs are finite; a program needn't handle non-finite values.
Results may differ from a plain program's by a relative error of at most 0.00012.
Values sent between devices are 32-bit elements; how exact they have to be, the bound alone decides.
A program may use at most 32 MiB of HBM per device.

v0:
```python
import jax
import jax.numpy as jnp
import numpy as np
from jax import lax
from jax.sharding import PartitionSpec as P

time_step = 2e-05
alpha_coef = -5.0 / 9.0
beta_coef = 15.0 / 16.0
lorentz_rate = 25.0
wave_step = 0.5


def cheb_matrix(points):
    intervals = points - 1
    index = np.arange(points)
    nodes = np.cos(np.pi * index / intervals)
    signs = np.ones(points)
    signs[0] = 2.0
    signs[-1] = 2.0
    signs = signs * (-1.0) ** index
    spread = nodes[:, None] - nodes[None, :]
    matrix = signs[:, None] / signs[None, :] / (spread + np.eye(points))
    matrix = matrix - np.eye(points) * matrix.sum(axis=1)[:, None]
    return matrix


def quad_weights(points):
    index = np.arange(points)
    return np.pi / (points - 1) * np.sin(np.pi * index / (points - 1))


def shards(perturb, register, ref_velocity):
    highest = lax.Precision.HIGHEST
    ref_a = lax.all_gather(ref_velocity, "member", axis=2, tiled=True)
    local_y = ref_a.shape[1]
    depth = ref_a.shape[2]
    channels = perturb.shape[2]
    slab = register.shape[1]
    span = register.shape[2] // channels
    waves_count = channels // 6
    members = lax.axis_size("member")
    dz_mat = jnp.asarray(cheb_matrix(depth), jnp.float32)
    dy_mat = jnp.asarray(cheb_matrix(span), jnp.float32)
    field_a = perturb[0]
    dzq = jnp.dot(field_a.reshape(-1, depth), dz_mat.T, precision=highest).reshape(
        local_y, waves_count, 2, 3, depth
    )
    dz_ref = jnp.dot(ref_a.reshape(-1, depth), dz_mat.T, precision=highest).reshape(
        3, local_y, depth
    )
    vel_w = ref_a[2]
    five_a = field_a.reshape(local_y, waves_count, 2, 3, depth)
    dz_ref_b = jnp.transpose(dz_ref, (1, 0, 2))[:, None, None, :, :]
    zpart = -vel_w[:, None, None, None, :] * dzq - five_a[:, :, :, 2:3] * dz_ref_b
    ref_part = -vel_w[None] * dz_ref
    packed = jnp.concatenate(
        [
            field_a,
            zpart.reshape(local_y, channels, depth),
            jnp.transpose(ref_a, (1, 0, 2)),
            jnp.transpose(ref_part, (1, 0, 2)),
        ],
        axis=1,
    )
    moved = lax.all_to_all(packed, "space", split_axis=2, concat_axis=0, tiled=True)
    field_b = moved[:, :channels]
    zpart_b = moved[:, channels : 2 * channels].reshape(span, waves_count, 2, 3, slab)
    ref_b = moved[:, 2 * channels : 2 * channels + 3]
    ref_zpart = moved[:, 2 * channels + 3 :]
    dyq = jnp.dot(dy_mat, field_b.reshape(span, -1), precision=highest).reshape(
        span, waves_count, 2, 3, slab
    )
    dy_ref = jnp.dot(dy_mat, ref_b.reshape(span, -1), precision=highest).reshape(span, 3, slab)
    five = field_b.reshape(span, waves_count, 2, 3, slab)
    stream_u = ref_b[:, 0][:, None, None, :]
    vel_v = ref_b[:, 1][:, None, None, None, :]
    waves = ((jnp.arange(waves_count) + 1).astype(jnp.float32) * wave_step).reshape(
        1, waves_count, 1, 1
    )
    lorentz = jnp.array([1.0, 0.0, 1.0], jnp.float32).reshape(1, 1, 1, 3, 1)
    twist = jnp.stack([waves * stream_u * five[:, :, 1], -waves * stream_u * five[:, :, 0]], axis=2)
    dy_ref_b = dy_ref[:, None, None, :, :]
    rhs = zpart_b + (
        -vel_v * dyq + twist - five[:, :, :, 1:2] * dy_ref_b - lorentz_rate * lorentz * five
    )
    row_index = jnp.arange(span)
    mask_y = ((row_index > 0) & (row_index < span - 1)).astype(jnp.float32)
    global_z = lax.axis_index("space") * slab + jnp.arange(slab)
    mask_z = ((global_z > 0) & (global_z < depth - 1)).astype(jnp.float32)
    mask_two = mask_y[:, None] * mask_z[None, :]
    mask_five = mask_two[:, None, None, None, :]
    reg_std = jnp.transpose(register[0].reshape(slab, span, channels), (1, 2, 0)).reshape(
        span, waves_count, 2, 3, slab
    )
    acc_new = mask_five * (alpha_coef * reg_std + time_step * rhs)
    field_new = mask_five * (five + beta_coef * acc_new)
    advanced = field_new.reshape(span, channels, slab)
    advanced_acc = acc_new.reshape(span, channels, slab)
    lorentz_three = jnp.array([1.0, 0.0, 1.0], jnp.float32).reshape(1, 3, 1)
    ref_full = (
        time_step
        * mask_two[:, None, :]
        * (ref_zpart + (-ref_b[:, 1:2] * dy_ref - lorentz_rate * lorentz_three * ref_b))
    )
    share = span // members
    ref_rows = lax.dynamic_slice_in_dim(ref_full, lax.axis_index("member") * share, share, 0)
    ref_step = jnp.transpose(ref_rows, (1, 0, 2))
    weight_y = jnp.asarray(quad_weights(span), jnp.float32)
    weight_all_z = jnp.asarray(quad_weights(depth), jnp.float32)
    weight_z = lax.dynamic_slice_in_dim(weight_all_z, lax.axis_index("space") * slab, slab, 0)
    weighted = advanced * weight_y[:, None, None] * weight_z[None, None, :]
    values = jnp.einsum(
        "mycz,ycz->m",
        lax.all_gather(advanced[None], "member", axis=0, tiled=True),
        weighted,
        precision=highest,
    )
    row = lax.dynamic_update_slice_in_dim(
        jnp.zeros((members,), jnp.float32), values, jnp.int32(0), 0
    )
    row = lax.psum(row, "space") / channels
    gram_row = row[None]
    advanced_out = jnp.transpose(advanced, (2, 0, 1)).reshape(slab, span * channels)
    acc_out = jnp.transpose(advanced_acc, (2, 0, 1)).reshape(slab, span * channels)
    return (advanced_out[None], acc_out[None], ref_step, gram_row)


def solution(mesh):
    return jax.shard_map(
        shards,
        mesh=mesh,
        in_specs=(
            P("member", "space", None, None),
            P("member", "space", None),
            P(None, "space", "member"),
        ),
        out_specs=(
            P("member", "space", None),
            P("member", "space", None),
            P(None, "member", "space"),
            P("member", None),
        ),
        check_vma=False,
    )
```

profile of v0, /device:TPU:387, one launch (start us, length us, event | category | flops | bytes accessed | tf_op | source)
XLA Modules:
  0.0 359.4 jit_solution(5606058205313239698)
XLA Ops:
  7.2 0.8 copy.96
  8.0 37.1 %all_gather.6 = f32[3,4,192]{1,0,2:T(4,128)S(1)} all-gather(f32[3,4,12]{1,0,2:T(4,128)S(1)} %copy.96), channel_id=1, replica_groups=mesh['member'=16,'space'=48] {'member'}, dimensions={2}, use_global_device_ids=true | all-gather | bytes 9792 | tf_op jit(solution)/shard_map/all_gather | solution.py:35
  45.6 1.2 broadcast_multiply_fusion.4
  46.8 1.3 copy.145
  48.1 1.5 fusion.1
  50.1 1.3 copy.106
  51.4 18.9 %all-to-all-start = ((f32[4,198,192]{1,0,2:T(4,128)}), f32[4,198,192]{1,0,2:T(4,128)S(1)}, u32[]{:S(2)}, u32[]{:S(2)}) async-start(f32[4,198,192]{1,0,2:T(4,128)} %copy.106), calls=%async_computation | async-start | bytes 1572864 | tf_op jit(solution)/shard_map/all_to_all | solution.py:66
  70.7 0.8 copy.94
  72.8 19.8 %all-to-all-done = f32[4,198,192]{1,0,2:T(4,128)S(1)} async-done(((f32[4,198,192]{1,0,2:T(4,128)}), f32[4,198,192]{1,0,2:T(4,128)S(1)}, u32[]{:S(2)}, u32[]{:S(2)}) %all-to-all-start) | async-done | bytes 608288 | tf_op jit(solution)/shard_map/all_to_all | solution.py:66
  93.4 1.2 fusion.12
  95.6 1.2 fusion.14
  96.9 1.1 reshape.192
  98.8 0.8 broadcast_multiply_fusion.3
  100.2 1.2 fusion.15
  101.4 1.0 broadcast_multiply_fusion
  102.6 3.0 multiply_bitcast_fusion
  105.7 0.7 constant_dynamic-slice_fusion
  106.6 1.0 broadcast_in_dim_reshape.9
  107.6 1.0 copy.121
  108.7 1.0 broadcast_in_dim_reshape.8
  109.8 0.7 fusion.9
  110.5 132.9 %all-gather.3.cloned.1.call-done = f32[3072,96,4]{1,2,0:T(4,128)} async-done(((f32[192,96,4]{1,2,0:T(4,128)}), f32[3072,96,4]{1,2,0:T(4,128)}) %all-gather.3.cloned.1.call-update) | async-done | bytes 4718608 | tf_op jit(solution)/shard_map/all_gather | solution.py:115
  243.3 4.7 %multiply_reduce_fusion = f32[16]{0:T(128)S(1)} fusion(f32[96,192,4,16]{0,2,1,3:T(4,128)} %bitcast.66, f32[96,192,4]{0,2,1:T(4,128)S(1)} %get-tuple-element.16), kind=kLoop, calls=%fused_computation | loop fusion | flops 2359280 | bytes 5013568 | tf_op jit(solution)/shard_map/mycz,ycz->m/dot_general | solution.py:113
  248.0 104.0 %psum.7 = f32[16]{0:T(128)S(1)} all-reduce(f32[16]{0:T(128)S(1)} %multiply_reduce_fusion), channel_id=1, replica_groups=mesh['member'=16,'space'=48] {'space'}, use_global_device_ids=true, to_apply=%region_0.0 | all-reduce | flops 16 | bytes 128 | tf_op jit(solution)/shard_map/psum | solution.py:122
  (49 shorter events, 6.7 us)
Async XLA Ops:
  7.2 63.3 %copy-start.2 = (f32[3]{0:T(128)S(1)}, f32[3]{0:T(128)}, u32[]{:S(2)}) copy-start(f32[3]{0:T(128)} %constant.48) | copy-start | bytes 40
  7.2 64.5 %copy-start.3 = (f32[192]{0:T(256)S(1)}, f32[192]{0:T(256)}, u32[]{:S(2)}) copy-start(f32[192]{0:T(256)} %constant.15.clone) | copy-start | bytes 2308
  7.2 63.2 %copy-start.1 = (f32[1,4,18432]{2,1,0:T(4,128)S(1)}, f32[1,4,18432]{2,1,0:T(4,128)}, u32[]{:S(2)}) copy-start(f32[1,4,18432]{2,1,0:T(4,128)} %param.10) | copy-start | bytes 884740
  50.1 45.5 %copy-start = (f32[192,192]{1,0:T(8,128)S(1)}, f32[192,192]{1,0:T(8,128)}, u32[]{:S(2)}) copy-start(f32[192,192]{1,0:T(8,128)} %constant.13.clone) | copy-start | bytes 442372
  51.4 41.2 %all-to-all-start = ((f32[4,198,192]{1,0,2:T(4,128)}), f32[4,198,192]{1,0,2:T(4,128)S(1)}, u32[]{:S(2)}, u32[]{:S(2)}) async-start(f32[4,198,192]{1,0,2:T(4,128)} %copy.106), calls=%async_computation | async-start | bytes 1572864 | tf_op jit(solution)/shard_map/all_to_all | solution.py:66
  70.3 173.0 %all-gather.3.cloned.1.call-start = ((), (), s32[]{:S(2)}) async-start(), calls=%async_computation.1 | async-start | bytes 6684672 | tf_op jit(solution)/shard_map/all_gather | solution.py:115
Sparse Core Ops, SparseCore 0:
  105.8 137.4 all-gather.2
where the time goes:
time: 360 us; the launch traced here: 359 us
  waiting for transfers between devices  153 us (42%)
  blocking collectives  141 us (39%)
  starting transfers between devices  18.9 us (5%)
  local copies, waits for them, and re-layouts  15.3 us (4%)
  between operations  14.3 us (4%)
  other arithmetic  11.8 us (3%)
  matrix products  5.12 us (1%)
    all_gather x1, waiting for transfers between devices, shards(): lax.all_gather(advanced[None], 'member', axis=0, tiled=True)  133 us
    psum x1, blocking collectives, shards(): row = lax.psum(row, 'space') / channels  104 us
    all_gather x1, blocking collectives, shards(): ref_a = lax.all_gather(ref_velocity, 'member', axis=2, tiled=True)  37.1 us
    all_to_all x1, waiting for transfers between devices, shards(): lax.all_to_all(packed, 'space', split_axis=2, concat_axis=0, tiled=True)  19.8 us
    all_to_all x1, starting transfers between devices, shards(): lax.all_to_all(packed, 'space', split_axis=2, concat_axis=0, tiled=True)  18.9 us
  transfers between devices with their start and end apart: 2, of which 2 were waited for; matrix products, arithmetic and copies ran while one was open for 2% of the time, Pallas kernels for 0%

commit v1 on v0

v1 whole, which is shorter than its diff:
```python
import functools

import jax
import jax.numpy as jnp
import numpy as np
from jax import lax
from jax.experimental import pallas as pl
from jax.experimental.pallas import tpu as pltpu
from jax.sharding import PartitionSpec as P

MESH = pl.DeviceIdType.MESH
HIGHEST = lax.Precision.HIGHEST

time_step = 2e-05
alpha_coef = -5.0 / 9.0
beta_coef = 15.0 / 16.0
lorentz_rate = 25.0
wave_step = 0.5

CH = 96
LANES = 128
SLOT = 40


def cheb_matrix(points):
    intervals = points - 1
    index = np.arange(points)
    nodes = np.cos(np.pi * index / intervals)
    signs = np.ones(points)
    signs[0] = 2.0
    signs[-1] = 2.0
    signs = signs * (-1.0) ** index
    spread = nodes[:, None] - nodes[None, :]
    matrix = signs[:, None] / signs[None, :] / (spread + np.eye(points))
    matrix = matrix - np.eye(points) * matrix.sum(axis=1)[:, None]
    return matrix


def quad_weights(points):
    index = np.arange(points)
    return np.pi / (points - 1) * np.sin(np.pi * index / (points - 1))


def constants(space, members):
    points = 4 * space
    diff = cheb_matrix(points).astype(np.float32)
    both = np.stack([np.eye(points, dtype=np.float32), diff]).reshape(2, space, 4, points)
    both = both.transpose(1, 0, 2, 3).reshape(2 * points, points)
    weight = quad_weights(points)
    lane_y = np.repeat(weight, CH).reshape(members, 9, LANES)
    lane_w = np.zeros((members, 16, LANES), np.float32)
    lane_w[:, :9] = lane_y
    return both, diff, lane_w, weight.astype(np.float32)


def mm(a, b, transpose_b=False):
    dims = (((1,), (1 if transpose_b else 0,)), ((), ()))
    return lax.dot_general(a, b, dims, precision=HIGHEST, preferred_element_type=jnp.float32)


def iota(shape, axis):
    return lax.broadcasted_iota(jnp.int32, shape, axis)


def kernel(
    S,
    M,
    p_ref,
    reg_ref,
    v_ref,
    a_ref,
    dy_ref,
    wl_ref,
    wz_ref,
    outf_ref,
    outa_ref,
    outr_ref,
    outg_ref,
    send_b,
    recv_b,
    tpose,
    own_x,
    gath_x,
    xz,
    ct,
    send_c,
    recv_c,
    coef,
    sbuf,
    tbuf,
    rbuf,
    f_loc,
    a_loc,
    f_buf,
    g_buf,
    gp,
    gr,
    row,
    rows,
    send_sem,
    recv_sem,
    out_sem,
):
    N = 4 * S
    H = S // 2
    m = lax.axis_index("member")
    s = lax.axis_index("space")

    def over_space(body):
        def step(k, carry):
            body(lax.rem(s + k, S))
            return carry

        lax.fori_loop(1, S, step, 0)

    def over_member(body):
        def step(k, carry):
            body(lax.rem(m + k, M))
            return carry

        lax.fori_loop(1, M, step, 0)

    def push(src, dst, which, member, space):
        pltpu.make_async_remote_copy(
            src_ref=src,
            dst_ref=dst,
            send_sem=send_sem.at[which],
            recv_sem=recv_sem.at[which],
            device_id=(member, space),
            device_id_type=MESH,
        ).start()

    def keep(src, dst, which):
        pltpu.make_async_copy(src, dst, recv_sem.at[which]).start()

    def arrived(ref, which):
        pltpu.make_async_copy(ref, ref, recv_sem.at[which]).wait()

    def sent(ref, which):
        pltpu.make_async_copy(ref, ref, send_sem.at[which]).wait()

    barrier = pltpu.get_barrier_semaphore()
    over_space(
        lambda t: pl.semaphore_signal(barrier, inc=1, device_id=(m, t), device_id_type=MESH)
    )
    over_member(
        lambda t: pl.semaphore_signal(barrier, inc=1, device_id=(t, s), device_id_type=MESH)
    )

    tpose[...] = jnp.zeros((LANES, LANES), jnp.float32)
    for c in range(3):
        tpose[4 * c : 4 * c + 4, 0:12] = v_ref[c]
    tpose[...] = tpose[...].T
    own_x[...] = (
        tpose[0:4, :]
        + pltpu.roll(tpose[4:8, :], 12, 1)
        + pltpu.roll(tpose[8:12, :], 24, 1)
    )
    send_b[...] = mm(a_ref[...], p_ref[...], transpose_b=True)

    pl.semaphore_wait(barrier, S - 1 + M - 1)

    over_member(lambda t: push(own_x, gath_x.at[m], 0, t, s))
    keep(own_x, gath_x.at[m], 0)

    def bulk(t):
        push(
            send_b.at[pl.ds(pl.multiple_of(8 * t, 8), 8), :],
            recv_b.at[pl.ds(pl.multiple_of(8 * s, 8), 8), :],
            1,
            m,
            t,
        )

    over_space(bulk)
    mine = pl.ds(pl.multiple_of(8 * s, 8), 8)
    keep(send_b.at[mine, :], recv_b.at[mine, :], 1)

    arrived(gath_x, 0)
    for k in range(M):
        piece = gath_x[k]
        for j in range(3):
            part = piece if j == 0 else pltpu.roll(piece, LANES - 12 * j, 1)
            xz[12 * k + 4 * j : 12 * k + 4 * j + 4, :] = part
    x = jnp.where(iota((N, LANES), 1) < 12, xz[...], 0.0)
    ct[...] = mm(a_ref[...], x)
    packed = ct[pl.ds(0, S, stride=8), :]
    for k in range(1, 8):
        packed = packed + pltpu.roll(ct[pl.ds(k, S, stride=8), :], 12 * k, 1)
    send_c[:, 0, :] = packed
    over_space(lambda t: push(send_c.at[t], recv_c.at[s], 2, m, t))
    keep(send_c.at[s], recv_c.at[s], 2)

    arrived(recv_c, 2)
    spread = (iota((N, S), 0) // 4 == iota((N, S), 1)).astype(jnp.float32)
    wide = mm(spread, recv_c[:, 0, :])
    points = jnp.where(iota((N, LANES), 1) % 4 == iota((N, LANES), 0) % 4, wide, 0.0)
    dpoints = mm(dy_ref[...], points)
    group = iota((LANES, LANES), 0) // 4
    lane = iota((LANES, LANES), 1)
    comp = lane % 3
    kx = wave_step * (lane // 6 + 1).astype(jnp.float32)
    kx = jnp.where(lane % 6 < 3, kx, -kx)
    lane_n = iota((N, LANES), 1)
    lorentz = jnp.where(lane_n % 3 == 1, 0.0, lorentz_rate)
    pick = (iota((16, N), 1) == 12 * m + iota((16, N), 0)).astype(jnp.float32)
    ref_rows = jnp.zeros((16, LANES), jnp.float32)
    for z in range(4):
        sel = [
            (group == 3 * z + 2).astype(jnp.float32),
            (group == 3 * z + 1).astype(jnp.float32),
            jnp.where(group == 3 * z, kx, 0.0),
            (group == 12 + 3 * z + comp).astype(jnp.float32),
            (group == 3 * z + comp).astype(jnp.float32),
        ]
        cw = mm(points, sel[0])
        cv = mm(points, sel[1])
        cu = mm(points, sel[2])
        cz = mm(points, sel[3])
        cr = mm(points, sel[4])
        cy = mm(dpoints, sel[4])
        coef[0, z] = cw
        coef[1, z] = cv
        coef[2, z] = cu
        coef[3, z] = cz
        coef[4, z] = cy
        ref_rhs = -cw * cz + (-cv * cy - lorentz * cr)
        got = mm(pick, ref_rhs)
        ref_rows = ref_rows + pltpu.roll(jnp.where(iota((16, LANES), 1) < 3, got, 0.0), 4 * z, 1)
    tpose[...] = jnp.zeros((LANES, LANES), jnp.float32)
    tpose[0:16, :] = ref_rows
    tpose[...] = tpose[...].T
    y_row = 12 * m + iota((1, 12), 1)
    for z in range(4):
        z_row = 4 * s + z
        inside = (y_row > 0) & (y_row < N - 1) & (z_row > 0) & (z_row < N - 1)
        for c in range(3):
            value = tpose[4 * z + c : 4 * z + c + 1, 0:12]
            outr_ref[c, z : z + 1, :] = time_step * jnp.where(inside, value, 0.0)

    arrived(recv_b, 1)
    lane8 = iota((8, LANES), 1)

    def expand(r, carry):
        base = pl.ds(pl.multiple_of(8 * r, 8), 8)
        v0 = recv_b[base, 0:128]
        v1 = recv_b[base, 128:256]
        v2 = recv_b[base, 256:384]
        y1 = jnp.where(lane8 < 32, pltpu.roll(v0, 32, 1), pltpu.roll(v1, 32, 1))
        y2 = jnp.where(lane8 < 64, pltpu.roll(v1, 64, 1), pltpu.roll(v2, 64, 1))
        y3 = pltpu.roll(v2, 96, 1)
        for i, v in enumerate((v0, y1, y2, y3)):
            sbuf[pl.ds(pl.multiple_of(32 * r + 8 * i, 8), 8), :] = v
        return carry

    lax.fori_loop(0, S, expand, 0)
    real = lane_n % 6 < 3
    comp_n = lane_n % 3
    half = N // 2
    for pair in range(2):
        q2 = jnp.concatenate(
            [sbuf[pl.ds(2 * pair + i, N, stride=8), :] for i in range(2)], axis=1
        )
        dyq2 = mm(dy_ref[...], q2)
        for i in range(2):
            z = 2 * pair + i
            q = q2[:, LANES * i : LANES * (i + 1)]
            dyq = dyq2[:, LANES * i : LANES * (i + 1)]
            dzq = sbuf[pl.ds(4 + z, N, stride=8), :]
            up1 = pltpu.roll(q, LANES - 1, 1)
            up2 = pltpu.roll(q, LANES - 2, 1)
            down1 = pltpu.roll(q, 1, 1)
            qz = jnp.where(comp_n == 0, up2, jnp.where(comp_n == 1, up1, q))
            qy = jnp.where(comp_n == 0, up1, jnp.where(comp_n == 1, q, down1))
            other = jnp.where(real, pltpu.roll(q, LANES - 3, 1), pltpu.roll(q, 3, 1))
            rhs = (-coef[0, z] * dzq - qz * coef[3, z]) + (
                -coef[1, z] * dyq + coef[2, z] * other - qy * coef[4, z] - lorentz * q
            )
            tbuf[pl.ds(z, half, stride=8), :] = rhs[0:half]
            tbuf[pl.ds(4 + z, half, stride=8), :] = rhs[half:N]

    def compact(r, carry):
        t = [tbuf[pl.ds(pl.multiple_of(32 * r + 8 * i, 8), 8), :] for i in range(4)]
        t1 = pltpu.roll(t[1], 96, 1)
        t2 = pltpu.roll(t[2], 64, 1)
        t3 = pltpu.roll(t[3], 32, 1)
        rbuf[r, :, 0:128] = jnp.where(lane8 < 96, t[0], t1)
        rbuf[r, :, 128:256] = jnp.where(lane8 < 64, t1, t2)
        rbuf[r, :, 256:384] = jnp.where(lane8 < 32, t2, t3)
        return carry

    lax.fori_loop(0, H, compact, 0)
    z_rows = 4 * s + iota((4, 384), 0)
    z_mask = (z_rows > 0) & (z_rows < N - 1)
    lane_y = iota((4, 384), 1) // CH

    def finish(g, carry):
        for h in range(2):
            slot = h * (S // 6) + g
            base = pl.multiple_of(SLOT * slot, 8)
            for i in range(3):
                r = h * H + 3 * g + i
                at = pl.ds(pl.multiple_of(384 * r, 128), 384)
                y = 4 * r + lane_y
                mask = jnp.where(z_mask & (y > 0) & (y < N - 1), 1.0, 0.0)
                rhs = rbuf[3 * g + i, 4 * h : 4 * h + 4, :]
                q = recv_b[pl.ds(pl.multiple_of(8 * r, 8), 4), :]
                acc = mask * (alpha_coef * reg_ref[:, at] + time_step * rhs)
                field = mask * (q + beta_coef * acc)
                a_loc[:, at] = acc
                f_loc[:, at] = field
                for l in range(3):
                    f_buf[pl.ds(base + 12 * i + 4 * l, 4), :] = field[:, 128 * l : 128 * l + 128]
        return carry

    lax.fori_loop(0, S // 6, finish, 0)

    def slot_of(t):
        return pl.ds(pl.multiple_of(SLOT * t, 8), SLOT)

    over_member(lambda t: push(f_buf.at[slot_of(t), :], g_buf.at[slot_of(m), :], 3, t, s))
    keep(f_buf.at[slot_of(m), :], g_buf.at[slot_of(m), :], 3)
    out_f = pltpu.make_async_copy(f_loc, outf_ref, out_sem.at[0])
    out_a = pltpu.make_async_copy(a_loc, outa_ref, out_sem.at[1])
    out_f.start()
    out_a.start()
    gp[...] = jnp.zeros((M, 1, LANES), jnp.float32)
    arrived(g_buf, 3)
    left = []
    right = []
    for t in range(9):
        weight_y = wl_ref[m, t : t + 1, :]
        for z in range(4):
            value = g_buf[pl.ds(4 * t + z, M, stride=SLOT), :]
            right.append(value)
            left.append(value * (weight_y * wz_ref[4 * s + z]))
    part = mm(jnp.concatenate(left, axis=1), jnp.concatenate(right, axis=1), transpose_b=True)
    for k in range(M):
        gp[k, :, 0:M] = part[k : k + 1, :]
    over_member(lambda t: push(gp.at[t], gr.at[m], 4, t, s))
    keep(gp.at[m], gr.at[m], 4)
    arrived(gr, 4)
    row[...] = jnp.sum(gr[...], axis=0)
    over_space(lambda t: push(row, rows.at[s], 5, m, t))
    keep(row, rows.at[s], 5)
    arrived(rows, 5)
    outg_ref[...] = (jnp.sum(rows[...], axis=0) / CH)[:, 0:M]

    sent(gath_x.at[0 : M - 1], 0)
    sent(recv_b.at[0 : 8 * (S - 1), :], 1)
    sent(recv_c.at[0 : S - 1], 2)
    sent(g_buf.at[0 : SLOT * (M - 1), :], 3)
    sent(gr.at[0 : M - 1], 4)
    sent(rows.at[0 : S - 1], 5)
    out_f.wait()
    out_a.wait()


def shards(S, M, perturb, register, ref_velocity):
    N = 4 * S
    f32 = jnp.float32
    both, diff, lane_w, weight = constants(S, M)
    vmem = pl.BlockSpec(memory_space=pltpu.VMEM)
    smem = pl.BlockSpec(memory_space=pltpu.SMEM)
    hbm = pl.BlockSpec(memory_space=pl.ANY)
    outs = pl.pallas_call(
        functools.partial(kernel, S, M),
        out_shape=(
            jax.ShapeDtypeStruct((4, N * CH), f32),
            jax.ShapeDtypeStruct((4, N * CH), f32),
            jax.ShapeDtypeStruct((3, 4, 12), f32),
            jax.ShapeDtypeStruct((1, M), f32),
        ),
        in_specs=[vmem] * 6 + [smem],
        out_specs=(hbm, hbm, vmem, vmem),
        scratch_shapes=[
            pltpu.VMEM((2 * N, 384), f32),
            pltpu.VMEM((2 * N, 384), f32),
            pltpu.VMEM((LANES, LANES), f32),
            pltpu.VMEM((4, LANES), f32),
            pltpu.VMEM((M, 4, LANES), f32),
            pltpu.VMEM((N, LANES), f32),
            pltpu.VMEM((2 * N, LANES), f32),
            pltpu.VMEM((S, 1, LANES), f32),
            pltpu.VMEM((S, 1, LANES), f32),
            pltpu.VMEM((5, 4, N, LANES), f32),
            pltpu.VMEM((8 * N, LANES), f32),
            pltpu.VMEM((4 * N, LANES), f32),
            pltpu.VMEM((S // 2, 8, 384), f32),
            pltpu.VMEM((4, N * CH), f32),
            pltpu.VMEM((4, N * CH), f32),
            pltpu.VMEM((SLOT * M, LANES), f32),
            pltpu.VMEM((SLOT * M, LANES), f32),
            pltpu.VMEM((M, 1, LANES), f32),
            pltpu.VMEM((M, 1, LANES), f32),
            pltpu.VMEM((1, LANES), f32),
            pltpu.VMEM((S, 1, LANES), f32),
            pltpu.SemaphoreType.DMA((6,)),
            pltpu.SemaphoreType.DMA((6,)),
            pltpu.SemaphoreType.DMA((2,)),
        ],
        compiler_params=pltpu.CompilerParams(collective_id=0, has_side_effects=True),
        name="substep",
    )(
        perturb.reshape(4 * CH, N),
        register[0],
        ref_velocity,
        jnp.asarray(both),
        jnp.asarray(diff),
        jnp.asarray(lane_w),
        jnp.asarray(weight),
    )
    fields, acc, ref_step, gram = outs
    return fields[None], acc[None], jnp.transpose(ref_step, (0, 2, 1)), gram


def solution(mesh):
    return jax.shard_map(
        functools.partial(shards, mesh.shape["space"], mesh.shape["member"]),
        mesh=mesh,
        in_specs=(
            P("member", "space", None, None),
            P("member", "space", None),
            P(None, "space", "member"),
        ),
        out_specs=(
            P("member", "space", None),
            P("member", "space", None),
            P(None, "member", "space"),
            P("member", None),
        ),
        check_vma=False,
    )
```

time: 360 us -> 83.4 us (0.23)
  the two profiles are of different devices: /device:TPU:387 before, /device:TPU:1 now
where the time goes in v1:
time: 83.4 us; the launch traced here: 83.2 us
  Pallas kernels  79 us (95%)
  local copies, waits for them, and re-layouts  3.63 us (4%)
    pallas_call x1, Pallas kernels, shards(): pl.pallas_call(functools.partial(kernel, S, M), out_shape=(jax.ShapeDtype...  79 us
    unnamed x10, local copies, waits for them, and re-layouts  3.63 us

profile of v1, /device:TPU:1, one launch (start us, length us, event | category | flops | bytes accessed | tf_op | source)
XLA Modules:
  0.0 83.2 jit_solution(4530622106751011510)
XLA Ops:
  0.6 79.0 %substep.1 = (f32[4,18432]{1,0:T(4,128)}, f32[4,18432]{1,0:T(4,128)}, f32[3,4,12]{2,1,0:T(4,128)}, f32[1,16]{1,0:T(1,128)}) custom-call(f32[384,192]{1,0:T(8,128)} %bitcast.5, f32[4,18432]{1,0:T(4,128)} %bitcast.8, f32[3,4,12]{2,1,0:T(4,128)} %v_ref.1, f32[384,192]{1,0:T(8,128)} %constant.8.clone.a_ref, f32[192,192]{1,0:T(8,128)} %constant.9.clone.dy_ref, ...), custom_call_target="tpu_custom_call" | custom-call | tf_op jit(solution)/shard_map/substep/pallas_call | solution.py:366
  79.6 0.0 copy-start
  79.6 1.7 %copy.15 = f32[1,4,18432]{2,1,0:T(4,128)} copy(f32[1,4,18432]{2,1,0:T(4,128)} %bitcast.7) | data formatting | bytes 589824
  81.3 0.0 copy-done
  81.3 0.0 copy-start.1
  81.3 0.7 copy.16
  82.1 0.0 copy-done.1
  82.1 0.0 copy-start.2
  82.1 0.6 copy.17
  82.7 0.1 copy-done.2
  82.7 0.5 copy.18
Async XLA Ops:
  79.6 1.8 %copy-start = (f32[4,18432]{1,0:T(4,128)S(1)}, f32[4,18432]{1,0:T(4,128)}, u32[]{:S(2)}) copy-start(f32[4,18432]{1,0:T(4,128)} %get-tuple-element.9) | copy-start | bytes 884740
  81.3 0.7 copy-start.1
  82.1 0.7 copy-start.2

commit v2 on v1

--- a/solution.py
+++ b/solution.py
@@ -47,10 +47,12 @@
     both = np.stack([np.eye(points, dtype=np.float32), diff]).reshape(2, space, 4, points)
     both = both.transpose(1, 0, 2, 3).reshape(2 * points, points)
     weight = quad_weights(points)
-    lane_y = np.repeat(weight, CH).reshape(members, 9, LANES)
+    root = np.sqrt(np.maximum(weight, 0.0))
     lane_w = np.zeros((members, 16, LANES), np.float32)
-    lane_w[:, :9] = lane_y
-    return both, diff, lane_w, weight.astype(np.float32)
+    lane_w[:, :9] = np.repeat(root, CH).reshape(members, 9, LANES)
+    z_w = np.zeros((space, 8, LANES), np.float32)
+    z_w[:, :4] = root.reshape(space, 4, 1)
+    return both, diff, lane_w, z_w
 
 
 def mm(a, b, transpose_b=False):
@@ -58,6 +60,19 @@
     return lax.dot_general(a, b, dims, precision=HIGHEST, preferred_element_type=jnp.float32)
 
 
+def split(x):
+    hi = x.astype(jnp.bfloat16)
+    rest = x - hi.astype(jnp.float32)
+    mid = rest.astype(jnp.bfloat16)
+    lo = (rest - mid.astype(jnp.float32)).astype(jnp.bfloat16)
+    return hi, mid, lo
+
+
+def mm_exact(parts, b):
+    dot = lambda a: jnp.dot(a, b, preferred_element_type=jnp.float32)
+    return (dot(parts[2]) + dot(parts[1])) + dot(parts[0])
+
+
 def iota(shape, axis):
     return lax.broadcasted_iota(jnp.int32, shape, axis)
 
@@ -65,6 +80,17 @@
 def kernel(
     S,
     M,
+    p_hbm,
+    reg_hbm,
+    v_hbm,
+    a_hbm,
+    dy_hbm,
+    wl_hbm,
+    wz_hbm,
+    outf_ref,
+    outa_ref,
+    outr_ref,
+    outg_ref,
     p_ref,
     reg_ref,
     v_ref,
@@ -72,10 +98,8 @@
     dy_ref,
     wl_ref,
     wz_ref,
-    outf_ref,
-    outa_ref,
-    outr_ref,
-    outg_ref,
+    sel_p,
+    sel_d,
     send_b,
     recv_b,
     tpose,
@@ -100,6 +124,7 @@
     send_sem,
     recv_sem,
     out_sem,
+    in_sem,
 ):
     N = 4 * S
     H = S // 2
@@ -109,9 +134,11 @@
     def over_space(body):
         def step(k, carry):
             body(lax.rem(s + k, S))
+            body(lax.rem(s + S - k, S))
             return carry
 
-        lax.fori_loop(1, S, step, 0)
+        lax.fori_loop(1, H, step, 0)
+        body(lax.rem(s + H, S))
 
     def over_member(body):
         def step(k, carry):
@@ -139,15 +166,33 @@
     def sent(ref, which):
         pltpu.make_async_copy(ref, ref, send_sem.at[which]).wait()
 
+    loads = [
+        pltpu.make_async_copy(src, dst, in_sem.at[k])
+        for k, (src, dst) in enumerate(
+            (
+                (v_hbm, v_ref),
+                (p_hbm, p_ref),
+                (a_hbm, a_ref),
+                (dy_hbm, dy_ref),
+                (reg_hbm, reg_ref),
+                (wl_hbm.at[m], wl_ref),
+                (wz_hbm.at[s], wz_ref),
+            )
+        )
+    ]
+    for load in loads:
+        load.start()
+
     barrier = pltpu.get_barrier_semaphore()
+    over_member(
+        lambda t: pl.semaphore_signal(barrier, inc=1, device_id=(t, s), device_id_type=MESH)
+    )
     over_space(
         lambda t: pl.semaphore_signal(barrier, inc=1, device_id=(m, t), device_id_type=MESH)
     )
-    over_member(
-        lambda t: pl.semaphore_signal(barrier, inc=1, device_id=(t, s), device_id_type=MESH)
-    )
 
     tpose[...] = jnp.zeros((LANES, LANES), jnp.float32)
+    loads[0].wait()
     for c in range(3):
         tpose[4 * c : 4 * c + 4, 0:12] = v_ref[c]
     tpose[...] = tpose[...].T
@@ -156,25 +201,51 @@
         + pltpu.roll(tpose[4:8, :], 12, 1)
         + pltpu.roll(tpose[8:12, :], 24, 1)
     )
+    loads[1].wait()
+    loads[2].wait()
     send_b[...] = mm(a_ref[...], p_ref[...], transpose_b=True)
+    group = iota((LANES, LANES), 0) // 4
+    lane = iota((LANES, LANES), 1)
+    comp = lane % 3
+    kx = wave_step * (lane // 6 + 1).astype(jnp.float32)
+    kx = jnp.where(lane % 6 < 3, kx, -kx)
+    for z in range(4):
+        chosen = [
+            (group == 3 * z + 2).astype(jnp.float32),
+            (group == 3 * z + 1).astype(jnp.float32),
+            jnp.where(group == 3 * z, kx, 0.0),
+            (group == 12 + 3 * z + comp).astype(jnp.float32),
+        ]
+        for k in range(4):
+            sel_p[z, :, LANES * k : LANES * (k + 1)] = chosen[k].astype(jnp.bfloat16)
+        sel_d[:, LANES * z : LANES * (z + 1)] = (
+            (group == 3 * z + comp).astype(jnp.float32).astype(jnp.bfloat16)
+        )
+    for load in loads[3:]:
+        load.wait()
 
     pl.semaphore_wait(barrier, S - 1 + M - 1)
 
     over_member(lambda t: push(own_x, gath_x.at[m], 0, t, s))
     keep(own_x, gath_x.at[m], 0)
 
-    def bulk(t):
-        push(
-            send_b.at[pl.ds(pl.multiple_of(8 * t, 8), 8), :],
-            recv_b.at[pl.ds(pl.multiple_of(8 * s, 8), 8), :],
-            1,
-            m,
-            t,
-        )
-
-    over_space(bulk)
-    mine = pl.ds(pl.multiple_of(8 * s, 8), 8)
-    keep(send_b.at[mine, :], recv_b.at[mine, :], 1)
+    def bulk(first, last, which):
+        mine = pl.ds(pl.multiple_of(8 * s, 8), 8)
+        lanes = slice(first, last)
+
+        def one(t):
+            push(
+                send_b.at[pl.ds(pl.multiple_of(8 * t, 8), 8), lanes],
+                recv_b.at[mine, lanes],
+                which,
+                m,
+                t,
+            )
+
+        over_space(one)
+        keep(send_b.at[mine, lanes], recv_b.at[mine, lanes], which)
+
+    bulk(0, 256, 1)
 
     arrived(gath_x, 0)
     for k in range(M):
@@ -190,70 +261,70 @@
     send_c[:, 0, :] = packed
     over_space(lambda t: push(send_c.at[t], recv_c.at[s], 2, m, t))
     keep(send_c.at[s], recv_c.at[s], 2)
+    bulk(256, 384, 6)
 
     arrived(recv_c, 2)
     spread = (iota((N, S), 0) // 4 == iota((N, S), 1)).astype(jnp.float32)
     wide = mm(spread, recv_c[:, 0, :])
     points = jnp.where(iota((N, LANES), 1) % 4 == iota((N, LANES), 0) % 4, wide, 0.0)
     dpoints = mm(dy_ref[...], points)
-    group = iota((LANES, LANES), 0) // 4
-    lane = iota((LANES, LANES), 1)
-    comp = lane % 3
-    kx = wave_step * (lane // 6 + 1).astype(jnp.float32)
-    kx = jnp.where(lane % 6 < 3, kx, -kx)
+    parts = split(points)
+    spread_y = mm_exact(split(dpoints), sel_d[...])
+    for z in range(4):
+        spread_p = mm_exact(parts, sel_p[z])
+        for k in range(4):
+            coef[k, z] = spread_p[:, LANES * k : LANES * (k + 1)]
+        coef[4, z] = spread_y[:, LANES * z : LANES * (z + 1)]
     lane_n = iota((N, LANES), 1)
     lorentz = jnp.where(lane_n % 3 == 1, 0.0, lorentz_rate)
+
     pick = (iota((16, N), 1) == 12 * m + iota((16, N), 0)).astype(jnp.float32)
-    ref_rows = jnp.zeros((16, LANES), jnp.float32)
-    for z in range(4):
-        sel = [
-            (group == 3 * z + 2).astype(jnp.float32),
-            (group == 3 * z + 1).astype(jnp.float32),
-            jnp.where(group == 3 * z, kx, 0.0),
-            (group == 12 + 3 * z + comp).astype(jnp.float32),
-            (group == 3 * z + comp).astype(jnp.float32),
-        ]
-        cw = mm(points, sel[0])
-        cv = mm(points, sel[1])
-        cu = mm(points, sel[2])
-        cz = mm(points, sel[3])
-        cr = mm(points, sel[4])
-        cy = mm(dpoints, sel[4])
-        coef[0, z] = cw
-        coef[1, z] = cv
-        coef[2, z] = cu
-        coef[3, z] = cz
-        coef[4, z] = cy
-        ref_rhs = -cw * cz + (-cv * cy - lorentz * cr)
-        got = mm(pick, ref_rhs)
-        ref_rows = ref_rows + pltpu.roll(jnp.where(iota((16, LANES), 1) < 3, got, 0.0), 4 * z, 1)
+
+    def fold(x):
+        x = x + pltpu.roll(x, LANES - 1, 1)
+        return x + pltpu.roll(x, LANES - 2, 1)
+
+    here = fold(mm(pick, points))
+    there = fold(mm(pick, dpoints))
+    which = (iota((16, LANES), 1) // 4) % 3
+    back4 = pltpu.roll(here, LANES - 4, 1)
+    back8 = pltpu.roll(here, LANES - 8, 1)
+    on4 = pltpu.roll(here, 4, 1)
+    vel_w = jnp.where(which == 0, back8, jnp.where(which == 1, back4, here))
+    vel_v = jnp.where(which == 0, back4, jnp.where(which == 1, here, on4))
+    drag = jnp.where(which == 1, 0.0, lorentz_rate)
+    dz_here = pltpu.roll(here, LANES - 48, 1)
     tpose[...] = jnp.zeros((LANES, LANES), jnp.float32)
-    tpose[0:16, :] = ref_rows
+    tpose[0:16, :] = -vel_w * dz_here + (-vel_v * there - drag * here)
     tpose[...] = tpose[...].T
     y_row = 12 * m + iota((1, 12), 1)
     for z in range(4):
         z_row = 4 * s + z
         inside = (y_row > 0) & (y_row < N - 1) & (z_row > 0) & (z_row < N - 1)
         for c in range(3):
-            value = tpose[4 * z + c : 4 * z + c + 1, 0:12]
+            at = 12 * z + 4 * c
+            value = tpose[at : at + 1, 0:12]
             outr_ref[c, z : z + 1, :] = time_step * jnp.where(inside, value, 0.0)
 
-    arrived(recv_b, 1)
+    arrived(recv_b.at[:, 0:256], 1)
+    arrived(recv_b.at[:, 256:384], 6)
     lane8 = iota((8, LANES), 1)
 
-    def expand(r, carry):
-        base = pl.ds(pl.multiple_of(8 * r, 8), 8)
-        v0 = recv_b[base, 0:128]
-        v1 = recv_b[base, 128:256]
-        v2 = recv_b[base, 256:384]
-        y1 = jnp.where(lane8 < 32, pltpu.roll(v0, 32, 1), pltpu.roll(v1, 32, 1))
-        y2 = jnp.where(lane8 < 64, pltpu.roll(v1, 64, 1), pltpu.roll(v2, 64, 1))
-        y3 = pltpu.roll(v2, 96, 1)
-        for i, v in enumerate((v0, y1, y2, y3)):
-            sbuf[pl.ds(pl.multiple_of(32 * r + 8 * i, 8), 8), :] = v
+    def expand(step, carry):
+        for u in range(3):
+            r = 3 * step + u
+            base = pl.ds(pl.multiple_of(8 * r, 8), 8)
+            v0 = recv_b[base, 0:128]
+            v1 = recv_b[base, 128:256]
+            v2 = recv_b[base, 256:384]
+            y1 = jnp.where(lane8 < 32, pltpu.roll(v0, 32, 1), pltpu.roll(v1, 32, 1))
+            y2 = jnp.where(lane8 < 64, pltpu.roll(v1, 64, 1), pltpu.roll(v2, 64, 1))
+            y3 = pltpu.roll(v2, 96, 1)
+            for i, v in enumerate((v0, y1, y2, y3)):
+                sbuf[pl.ds(pl.multiple_of(32 * r + 8 * i, 8), 8), :] = v
         return carry
 
-    lax.fori_loop(0, S, expand, 0)
+    lax.fori_loop(0, S // 3, expand, 0)
     real = lane_n % 6 < 3
     comp_n = lane_n % 3
     half = N // 2
@@ -279,20 +350,25 @@
             tbuf[pl.ds(z, half, stride=8), :] = rhs[0:half]
             tbuf[pl.ds(4 + z, half, stride=8), :] = rhs[half:N]
 
-    def compact(r, carry):
-        t = [tbuf[pl.ds(pl.multiple_of(32 * r + 8 * i, 8), 8), :] for i in range(4)]
-        t1 = pltpu.roll(t[1], 96, 1)
-        t2 = pltpu.roll(t[2], 64, 1)
-        t3 = pltpu.roll(t[3], 32, 1)
-        rbuf[r, :, 0:128] = jnp.where(lane8 < 96, t[0], t1)
-        rbuf[r, :, 128:256] = jnp.where(lane8 < 64, t1, t2)
-        rbuf[r, :, 256:384] = jnp.where(lane8 < 32, t2, t3)
+    def compact(step, carry):
+        for u in range(3):
+            r = 3 * step + u
+            t = [tbuf[pl.ds(pl.multiple_of(32 * r + 8 * i, 8), 8), :] for i in range(4)]
+            t1 = pltpu.roll(t[1], 96, 1)
+            t2 = pltpu.roll(t[2], 64, 1)
+            t3 = pltpu.roll(t[3], 32, 1)
+            rbuf[r, :, 0:128] = jnp.where(lane8 < 96, t[0], t1)
+            rbuf[r, :, 128:256] = jnp.where(lane8 < 64, t1, t2)
+            rbuf[r, :, 256:384] = jnp.where(lane8 < 32, t2, t3)
         return carry
 
-    lax.fori_loop(0, H, compact, 0)
+    lax.fori_loop(0, H // 3, compact, 0)
     z_rows = 4 * s + iota((4, 384), 0)
     z_mask = (z_rows > 0) & (z_rows < N - 1)
     lane_y = iota((4, 384), 1) // CH
+
+    def slot_of(t):
+        return pl.ds(pl.multiple_of(SLOT * t, 8), SLOT)
 
     def finish(g, carry):
         for h in range(2):
@@ -311,14 +387,15 @@
                 f_loc[:, at] = field
                 for l in range(3):
                     f_buf[pl.ds(base + 12 * i + 4 * l, 4), :] = field[:, 128 * l : 128 * l + 128]
+
+            @pl.when(slot != m)
+            def _():
+                push(f_buf.at[slot_of(slot), :], g_buf.at[slot_of(m), :], 3, slot, s)
+
         return carry
 
     lax.fori_loop(0, S // 6, finish, 0)
 
-    def slot_of(t):
-        return pl.ds(pl.multiple_of(SLOT * t, 8), SLOT)
-
-    over_member(lambda t: push(f_buf.at[slot_of(t), :], g_buf.at[slot_of(m), :], 3, t, s))
     keep(f_buf.at[slot_of(m), :], g_buf.at[slot_of(m), :], 3)
     out_f = pltpu.make_async_copy(f_loc, outf_ref, out_sem.at[0])
     out_a = pltpu.make_async_copy(a_loc, outa_ref, out_sem.at[1])
@@ -326,15 +403,20 @@
     out_a.start()
     gp[...] = jnp.zeros((M, 1, LANES), jnp.float32)
     arrived(g_buf, 3)
-    left = []
-    right = []
+    values = []
     for t in range(9):
-        weight_y = wl_ref[m, t : t + 1, :]
+        weight_y = wl_ref[t : t + 1, :]
         for z in range(4):
             value = g_buf[pl.ds(4 * t + z, M, stride=SLOT), :]
-            right.append(value)
-            left.append(value * (weight_y * wz_ref[4 * s + z]))
-    part = mm(jnp.concatenate(left, axis=1), jnp.concatenate(right, axis=1), transpose_b=True)
+            values.append(split(value * (weight_y * wz_ref[z : z + 1, :])))
+    stack = jnp.concatenate(
+        [jnp.concatenate([v[k] for v in values], axis=1) for k in range(3)], axis=0
+    )
+    nine = lax.dot_general(
+        stack, stack, (((1,), (1,)), ((), ())), preferred_element_type=jnp.float32
+    )
+    three = (nine[2 * M : 3 * M] + nine[M : 2 * M]) + nine[0:M]
+    part = (three[:, 2 * M : 3 * M] + three[:, M : 2 * M]) + three[:, 0:M]
     for k in range(M):
         gp[k, :, 0:M] = part[k : k + 1, :]
     over_member(lambda t: push(gp.at[t], gr.at[m], 4, t, s))
@@ -347,7 +429,8 @@
     outg_ref[...] = (jnp.sum(rows[...], axis=0) / CH)[:, 0:M]
 
     sent(gath_x.at[0 : M - 1], 0)
-    sent(recv_b.at[0 : 8 * (S - 1), :], 1)
+    sent(recv_b.at[0 : 8 * (S - 1), 0:256], 1)
+    sent(recv_b.at[0 : 8 * (S - 1), 256:384], 6)
     sent(recv_c.at[0 : S - 1], 2)
     sent(g_buf.at[0 : SLOT * (M - 1), :], 3)
     sent(gr.at[0 : M - 1], 4)
@@ -356,12 +439,40 @@
     out_a.wait()
 
 
+def copy_kernel(*refs):
+    n = (len(refs) - 2) // 3
+    ins, outs, held = refs[:n], refs[n : 2 * n], refs[2 * n : 3 * n]
+    in_sem, out_sem = refs[3 * n :]
+    loads = [pltpu.make_async_copy(ins[k], held[k], in_sem.at[k]) for k in range(n)]
+    stores = [pltpu.make_async_copy(held[k], outs[k], out_sem.at[k]) for k in range(n)]
+    for load in loads:
+        load.start()
+    for load, store in zip(loads, stores):
+        load.wait()
+        store.start()
+    for store in stores:
+        store.wait()
+
+
+def handed_on(arrays):
+    hbm = pl.BlockSpec(memory_space=pl.ANY)
+    n = len(arrays)
+    return pl.pallas_call(
+        copy_kernel,
+        out_shape=[jax.ShapeDtypeStruct(a.shape, a.dtype) for a in arrays],
+        in_specs=[hbm] * n,
+        out_specs=[hbm] * n,
+        scratch_shapes=[pltpu.VMEM(a.shape, a.dtype) for a in arrays]
+        + [pltpu.SemaphoreType.DMA((n,)), pltpu.SemaphoreType.DMA((n,))],
+        name="hand_on",
+    )(*arrays)
+
+
 def shards(S, M, perturb, register, ref_velocity):
     N = 4 * S
     f32 = jnp.float32
-    both, diff, lane_w, weight = constants(S, M)
+    both, diff, lane_w, z_w = constants(S, M)
     vmem = pl.BlockSpec(memory_space=pltpu.VMEM)
-    smem = pl.BlockSpec(memory_space=pltpu.SMEM)
     hbm = pl.BlockSpec(memory_space=pl.ANY)
     outs = pl.pallas_call(
         functools.partial(kernel, S, M),
@@ -371,9 +482,18 @@
             jax.ShapeDtypeStruct((3, 4, 12), f32),
             jax.ShapeDtypeStruct((1, M), f32),
         ),
-        in_specs=[vmem] * 6 + [smem],
+        in_specs=[hbm] * 7,
         out_specs=(hbm, hbm, vmem, vmem),
         scratch_shapes=[
+            pltpu.VMEM((4 * CH, N), f32),
+            pltpu.VMEM((4, N * CH), f32),
+            pltpu.VMEM((3, 4, 12), f32),
+            pltpu.VMEM((2 * N, N), f32),
+            pltpu.VMEM((N, N), f32),
+            pltpu.VMEM((16, LANES), f32),
+            pltpu.VMEM((8, LANES), f32),
+            pltpu.VMEM((4, LANES, 4 * LANES), jnp.bfloat16),
+            pltpu.VMEM((LANES, 4 * LANES), jnp.bfloat16),
             pltpu.VMEM((2 * N, 384), f32),
             pltpu.VMEM((2 * N, 384), f32),
             pltpu.VMEM((LANES, LANES), f32),
@@ -395,9 +515,10 @@
             pltpu.VMEM((M, 1, LANES), f32),
             pltpu.VMEM((1, LANES), f32),
             pltpu.VMEM((S, 1, LANES), f32),
-            pltpu.SemaphoreType.DMA((6,)),
-            pltpu.SemaphoreType.DMA((6,)),
+            pltpu.SemaphoreType.DMA((7,)),
+            pltpu.SemaphoreType.DMA((7,)),
             pltpu.SemaphoreType.DMA((2,)),
+            pltpu.SemaphoreType.DMA((7,)),
         ],
         compiler_params=pltpu.CompilerParams(collective_id=0, has_side_effects=True),
         name="substep",
@@ -408,9 +529,9 @@
         jnp.asarray(both),
         jnp.asarray(diff),
         jnp.asarray(lane_w),
-        jnp.asarray(weight),
-    )
-    fields, acc, ref_step, gram = outs
+        jnp.asarray(z_w),
+    )
+    fields, acc, ref_step, gram = handed_on(outs)
     return fields[None], acc[None], jnp.transpose(ref_step, (0, 2, 1)), gram
 
 

time: 83.4 us -> 72.6 us (0.87)
  Pallas kernels: 79 us -> 71.8 us
  local copies, waits for them, and re-layouts: 3.63 us -> 0 us
    pallas_call x1, Pallas kernels: 79 us -> 70 us  [shards(): pl.pallas_call(functools.partial(kernel, S, M), out_shape=(jax.ShapeDtype...]
    unnamed x10 -> x0, local copies, waits for them, and re-layouts: 3.63 us -> none
    pallas_call x0 -> x1, Pallas kernels: none -> 1.85 us  [handed_on(): pl.pallas_call(copy_kernel, out_shape=[jax.ShapeDtypeStruct(a.shape, a.dt...]
where the time goes in v2:
time: 72.6 us; the launch traced here: 72.5 us
  Pallas kernels  71.8 us (99%)
    pallas_call x1, Pallas kernels, shards(): pl.pallas_call(functools.partial(kernel, S, M), out_shape=(jax.ShapeDtype...  70 us
    pallas_call x1, Pallas kernels, handed_on(): pl.pallas_call(copy_kernel, out_shape=[jax.ShapeDtypeStruct(a.shape, a.dt...  1.85 us

profile of v2, /device:TPU:1, one launch (start us, length us, event | category | flops | bytes accessed | tf_op | source)
XLA Modules:
  0.0 72.5 jit_solution(2200644793958062957)
XLA Ops:
  0.6 70.0 %substep.1 = (f32[4,18432]{1,0:T(4,128)}, f32[4,18432]{1,0:T(4,128)}, f32[3,4,12]{2,1,0:T(4,128)}, f32[1,16]{1,0:T(1,128)}) custom-call(f32[384,192]{1,0:T(8,128)} %bitcast.5, f32[4,18432]{1,0:T(4,128)} %bitcast.6, f32[3,4,12]{2,1,0:T(4,128)} %v_hbm.1, f32[384,192]{1,0:T(8,128)} %constant.8.clone.a_hbm, f32[192,192]{1,0:T(8,128)} %constant.9.clone.dy_hbm, ...), custom_call_target="tpu_custom_call" | custom-call | tf_op jit(solution)/shard_map/substep/pallas_call | solution.py:477
  70.6 1.8 %hand_on.1 = (f32[4,18432]{1,0:T(4,128)}, f32[4,18432]{1,0:T(4,128)}, f32[3,4,12]{2,1,0:T(4,128)}, f32[1,16]{1,0:T(1,128)}) custom-call(f32[4,18432]{1,0:T(4,128)} %get-tuple-element.12.refs_0_, f32[4,18432]{1,0:T(4,128)} %get-tuple-element.13.refs_1_, f32[3,4,12]{2,1,0:T(4,128)} %get-tuple-element.14.refs_2_, f32[1,16]{1,0:T(1,128)} %get-tuple-element.15.refs_3_), custom_call_target="tpu_custom_call" | custom-call | tf_op jit(solution)/shard_map/hand_on/pallas_call | solution.py:460

commit v3 on v2

--- a/solution.py
+++ b/solution.py
@@ -20,6 +20,7 @@
 CH = 96
 LANES = 128
 SLOT = 40
+USED = 36
 
 
 def cheb_matrix(points):
@@ -87,8 +88,8 @@
     dy_hbm,
     wl_hbm,
     wz_hbm,
-    outf_ref,
-    outa_ref,
+    f_loc,
+    a_loc,
     outr_ref,
     outg_ref,
     p_ref,
@@ -111,10 +112,9 @@
     recv_c,
     coef,
     sbuf,
+    dyq_b,
     tbuf,
     rbuf,
-    f_loc,
-    a_loc,
     f_buf,
     g_buf,
     gp,
@@ -123,7 +123,6 @@
     rows,
     send_sem,
     recv_sem,
-    out_sem,
     in_sem,
 ):
     N = 4 * S
@@ -204,6 +203,29 @@
     loads[1].wait()
     loads[2].wait()
     send_b[...] = mm(a_ref[...], p_ref[...], transpose_b=True)
+    pl.semaphore_wait(barrier, S - 1 + M - 1)
+
+    over_member(lambda t: push(own_x, gath_x.at[m], 0, t, s))
+    keep(own_x, gath_x.at[m], 0)
+
+    def bulk(first, last, which):
+        mine = pl.ds(pl.multiple_of(8 * s, 8), 8)
+        lanes = slice(first, last)
+
+        def one(t):
+            push(
+                send_b.at[pl.ds(pl.multiple_of(8 * t, 8), 8), lanes],
+                recv_b.at[mine, lanes],
+                which,
+                m,
+                t,
+            )
+
+        over_space(one)
+        keep(send_b.at[mine, lanes], recv_b.at[mine, lanes], which)
+
+    bulk(0, 256, 1)
+
     group = iota((LANES, LANES), 0) // 4
     lane = iota((LANES, LANES), 1)
     comp = lane % 3
@@ -224,29 +246,6 @@
     for load in loads[3:]:
         load.wait()
 
-    pl.semaphore_wait(barrier, S - 1 + M - 1)
-
-    over_member(lambda t: push(own_x, gath_x.at[m], 0, t, s))
-    keep(own_x, gath_x.at[m], 0)
-
-    def bulk(first, last, which):
-        mine = pl.ds(pl.multiple_of(8 * s, 8), 8)
-        lanes = slice(first, last)
-
-        def one(t):
-            push(
-                send_b.at[pl.ds(pl.multiple_of(8 * t, 8), 8), lanes],
-                recv_b.at[mine, lanes],
-                which,
-                m,
-                t,
-            )
-
-        over_space(one)
-        keep(send_b.at[mine, lanes], recv_b.at[mine, lanes], which)
-
-    bulk(0, 256, 1)
-
     arrived(gath_x, 0)
     for k in range(M):
         piece = gath_x[k]
@@ -254,19 +253,48 @@
             part = piece if j == 0 else pltpu.roll(piece, LANES - 12 * j, 1)
             xz[12 * k + 4 * j : 12 * k + 4 * j + 4, :] = part
     x = jnp.where(iota((N, LANES), 1) < 12, xz[...], 0.0)
-    ct[...] = mm(a_ref[...], x)
-    packed = ct[pl.ds(0, S, stride=8), :]
-    for k in range(1, 8):
-        packed = packed + pltpu.roll(ct[pl.ds(k, S, stride=8), :], 12 * k, 1)
+    xz[...] = x
+    ct[...] = mm(dy_ref[...], x)
+    packed = xz[pl.ds(0, S, stride=4), :]
+    for z in range(1, 4):
+        packed = packed + pltpu.roll(xz[pl.ds(z, S, stride=4), :], 12 * z, 1)
+    for z in range(4):
+        packed = packed + pltpu.roll(ct[pl.ds(z, S, stride=4), :], 48 + 12 * z, 1)
     send_c[:, 0, :] = packed
     over_space(lambda t: push(send_c.at[t], recv_c.at[s], 2, m, t))
     keep(send_c.at[s], recv_c.at[s], 2)
     bulk(256, 384, 6)
 
+    arrived(recv_b.at[:, 0:256], 1)
+    arrived(recv_b.at[:, 256:384], 6)
+    lane8 = iota((8, LANES), 1)
+
+    def expand(step, carry):
+        for u in range(3):
+            r = 3 * step + u
+            base = pl.ds(pl.multiple_of(8 * r, 8), 8)
+            v0 = recv_b[base, 0:128]
+            v1 = recv_b[base, 128:256]
+            v2 = recv_b[base, 256:384]
+            y1 = jnp.where(lane8 < 32, pltpu.roll(v0, 32, 1), pltpu.roll(v1, 32, 1))
+            y2 = jnp.where(lane8 < 64, pltpu.roll(v1, 64, 1), pltpu.roll(v2, 64, 1))
+            y3 = pltpu.roll(v2, 96, 1)
+            for i, v in enumerate((v0, y1, y2, y3)):
+                sbuf[pl.ds(pl.multiple_of(32 * r + 8 * i, 8), 8), :] = v
+        return carry
+
+    lax.fori_loop(0, S // 3, expand, 0)
+    for pair in range(2):
+        q2 = jnp.concatenate(
+            [sbuf[pl.ds(2 * pair + i, N, stride=8), :] for i in range(2)], axis=1
+        )
+        dyq_b[pair] = mm(dy_ref[...], q2)
+
     arrived(recv_c, 2)
-    spread = (iota((N, S), 0) // 4 == iota((N, S), 1)).astype(jnp.float32)
-    wide = mm(spread, recv_c[:, 0, :])
-    points = jnp.where(iota((N, LANES), 1) % 4 == iota((N, LANES), 0) % 4, wide, 0.0)
+    lane_s = iota((S, LANES), 1) % 4
+    for k in range(4):
+        xz[pl.ds(k, S, stride=4), :] = jnp.where(lane_s == k, recv_c[:, 0, :], 0.0)
+    points = xz[...]
     dpoints = mm(dy_ref[...], points)
     parts = split(points)
     spread_y = mm_exact(split(dpoints), sel_d[...])
@@ -275,9 +303,76 @@
         for k in range(4):
             coef[k, z] = spread_p[:, LANES * k : LANES * (k + 1)]
         coef[4, z] = spread_y[:, LANES * z : LANES * (z + 1)]
+
     lane_n = iota((N, LANES), 1)
     lorentz = jnp.where(lane_n % 3 == 1, 0.0, lorentz_rate)
 
+    real = lane_n % 6 < 3
+    comp_n = lane_n % 3
+    half = N // 2
+    for z in range(4):
+        q = sbuf[pl.ds(z, N, stride=8), :]
+        dzq = sbuf[pl.ds(4 + z, N, stride=8), :]
+        dyq = dyq_b[z // 2, :, LANES * (z % 2) : LANES * (z % 2 + 1)]
+        up1 = pltpu.roll(q, LANES - 1, 1)
+        up2 = pltpu.roll(q, LANES - 2, 1)
+        down1 = pltpu.roll(q, 1, 1)
+        qz = jnp.where(comp_n == 0, up2, jnp.where(comp_n == 1, up1, q))
+        qy = jnp.where(comp_n == 0, up1, jnp.where(comp_n == 1, q, down1))
+        other = jnp.where(real, pltpu.roll(q, LANES - 3, 1), pltpu.roll(q, 3, 1))
+        rhs = (-coef[0, z] * dzq - qz * coef[3, z]) + (
+            -coef[1, z] * dyq + coef[2, z] * other - qy * coef[4, z] - lorentz * q
+        )
+        tbuf[pl.ds(z, half, stride=8), :] = rhs[0:half]
+        tbuf[pl.ds(4 + z, half, stride=8), :] = rhs[half:N]
+
+    def compact(step, carry):
+        for u in range(3):
+            r = 3 * step + u
+            t = [tbuf[pl.ds(pl.multiple_of(32 * r + 8 * i, 8), 8), :] for i in range(4)]
+            t1 = pltpu.roll(t[1], 96, 1)
+            t2 = pltpu.roll(t[2], 64, 1)
+            t3 = pltpu.roll(t[3], 32, 1)
+            rbuf[r, :, 0:128] = jnp.where(lane8 < 96, t[0], t1)
+            rbuf[r, :, 128:256] = jnp.where(lane8 < 64, t1, t2)
+            rbuf[r, :, 256:384] = jnp.where(lane8 < 32, t2, t3)
+        return carry
+
+    lax.fori_loop(0, H // 3, compact, 0)
+    z_rows = 4 * s + iota((4, 384), 0)
+    z_mask = (z_rows > 0) & (z_rows < N - 1)
+    lane_y = iota((4, 384), 1) // CH
+
+    def slot_of(t):
+        return pl.ds(pl.multiple_of(SLOT * t, 8), USED)
+
+    def finish(g, carry):
+        for h in range(2):
+            slot = h * (S // 6) + g
+            base = pl.multiple_of(SLOT * slot, 8)
+            for i in range(3):
+                r = h * H + 3 * g + i
+                at = pl.ds(pl.multiple_of(384 * r, 128), 384)
+                y = 4 * r + lane_y
+                mask = jnp.where(z_mask & (y > 0) & (y < N - 1), 1.0, 0.0)
+                rhs = rbuf[3 * g + i, 4 * h : 4 * h + 4, :]
+                q = recv_b[pl.ds(pl.multiple_of(8 * r, 8), 4), :]
+                acc = mask * (alpha_coef * reg_ref[:, at] + time_step * rhs)
+                field = mask * (q + beta_coef * acc)
+                a_loc[:, at] = acc
+                f_loc[:, at] = field
+                for l in range(3):
+                    f_buf[pl.ds(base + 12 * i + 4 * l, 4), :] = field[:, 128 * l : 128 * l + 128]
+
+            @pl.when(slot != m)
+            def _():
+                push(f_buf.at[slot_of(slot), :], g_buf.at[slot_of(m), :], 3, slot, s)
+
+        return carry
+
+    lax.fori_loop(0, S // 6, finish, 0)
+
+    keep(f_buf.at[slot_of(m), :], g_buf.at[slot_of(m), :], 3)
     pick = (iota((16, N), 1) == 12 * m + iota((16, N), 0)).astype(jnp.float32)
 
     def fold(x):
@@ -306,103 +401,8 @@
             value = tpose[at : at + 1, 0:12]
             outr_ref[c, z : z + 1, :] = time_step * jnp.where(inside, value, 0.0)
 
-    arrived(recv_b.at[:, 0:256], 1)
-    arrived(recv_b.at[:, 256:384], 6)
-    lane8 = iota((8, LANES), 1)
-
-    def expand(step, carry):
-        for u in range(3):
-            r = 3 * step + u
-            base = pl.ds(pl.multiple_of(8 * r, 8), 8)
-            v0 = recv_b[base, 0:128]
-            v1 = recv_b[base, 128:256]
-            v2 = recv_b[base, 256:384]
-            y1 = jnp.where(lane8 < 32, pltpu.roll(v0, 32, 1), pltpu.roll(v1, 32, 1))
-            y2 = jnp.where(lane8 < 64, pltpu.roll(v1, 64, 1), pltpu.roll(v2, 64, 1))
-            y3 = pltpu.roll(v2, 96, 1)
-            for i, v in enumerate((v0, y1, y2, y3)):
-                sbuf[pl.ds(pl.multiple_of(32 * r + 8 * i, 8), 8), :] = v
-        return carry
-
-    lax.fori_loop(0, S // 3, expand, 0)
-    real = lane_n % 6 < 3
-    comp_n = lane_n % 3
-    half = N // 2
-    for pair in range(2):
-        q2 = jnp.concatenate(
-            [sbuf[pl.ds(2 * pair + i, N, stride=8), :] for i in range(2)], axis=1
-        )
-        dyq2 = mm(dy_ref[...], q2)
-        for i in range(2):
-            z = 2 * pair + i
-            q = q2[:, LANES * i : LANES * (i + 1)]
-            dyq = dyq2[:, LANES * i : LANES * (i + 1)]
-            dzq = sbuf[pl.ds(4 + z, N, stride=8), :]
-            up1 = pltpu.roll(q, LANES - 1, 1)
-            up2 = pltpu.roll(q, LANES - 2, 1)
-            down1 = pltpu.roll(q, 1, 1)
-            qz = jnp.where(comp_n == 0, up2, jnp.where(comp_n == 1, up1, q))
-            qy = jnp.where(comp_n == 0, up1, jnp.where(comp_n == 1, q, down1))
-            other = jnp.where(real, pltpu.roll(q, LANES - 3, 1), pltpu.roll(q, 3, 1))
-            rhs = (-coef[0, z] * dzq - qz * coef[3, z]) + (
-                -coef[1, z] * dyq + coef[2, z] * other - qy * coef[4, z] - lorentz * q
-            )
-            tbuf[pl.ds(z, half, stride=8), :] = rhs[0:half]
-            tbuf[pl.ds(4 + z, half, stride=8), :] = rhs[half:N]
-
-    def compact(step, carry):
-        for u in range(3):
-            r = 3 * step + u
-            t = [tbuf[pl.ds(pl.multiple_of(32 * r + 8 * i, 8), 8), :] for i in range(4)]
-            t1 = pltpu.roll(t[1], 96, 1)
-            t2 = pltpu.roll(t[2], 64, 1)
-            t3 = pltpu.roll(t[3], 32, 1)
-            rbuf[r, :, 0:128] = jnp.where(lane8 < 96, t[0], t1)
-            rbuf[r, :, 128:256] = jnp.where(lane8 < 64, t1, t2)
-            rbuf[r, :, 256:384] = jnp.where(lane8 < 32, t2, t3)
-        return carry
-
-    lax.fori_loop(0, H // 3, compact, 0)
-    z_rows = 4 * s + iota((4, 384), 0)
-    z_mask = (z_rows > 0) & (z_rows < N - 1)
-    lane_y = iota((4, 384), 1) // CH
-
-    def slot_of(t):
-        return pl.ds(pl.multiple_of(SLOT * t, 8), SLOT)
-
-    def finish(g, carry):
-        for h in range(2):
-            slot = h * (S // 6) + g
-            base = pl.multiple_of(SLOT * slot, 8)
-            for i in range(3):
-                r = h * H + 3 * g + i
-                at = pl.ds(pl.multiple_of(384 * r, 128), 384)
-                y = 4 * r + lane_y
-                mask = jnp.where(z_mask & (y > 0) & (y < N - 1), 1.0, 0.0)
-                rhs = rbuf[3 * g + i, 4 * h : 4 * h + 4, :]
-                q = recv_b[pl.ds(pl.multiple_of(8 * r, 8), 4), :]
-                acc = mask * (alpha_coef * reg_ref[:, at] + time_step * rhs)
-                field = mask * (q + beta_coef * acc)
-                a_loc[:, at] = acc
-                f_loc[:, at] = field
-                for l in range(3):
-                    f_buf[pl.ds(base + 12 * i + 4 * l, 4), :] = field[:, 128 * l : 128 * l + 128]
-
-            @pl.when(slot != m)
-            def _():
-                push(f_buf.at[slot_of(slot), :], g_buf.at[slot_of(m), :], 3, slot, s)
-
-        return carry
-
-    lax.fori_loop(0, S // 6, finish, 0)
-
-    keep(f_buf.at[slot_of(m), :], g_buf.at[slot_of(m), :], 3)
-    out_f = pltpu.make_async_copy(f_loc, outf_ref, out_sem.at[0])
-    out_a = pltpu.make_async_copy(a_loc, outa_ref, out_sem.at[1])
-    out_f.start()
-    out_a.start()
     gp[...] = jnp.zeros((M, 1, LANES), jnp.float32)
-    arrived(g_buf, 3)
+    arrived(g_buf.at[0 : USED * M, :], 3)
     values = []
     for t in range(9):
         weight_y = wl_ref[t : t + 1, :]
@@ -432,38 +432,29 @@
     sent(recv_b.at[0 : 8 * (S - 1), 0:256], 1)
     sent(recv_b.at[0 : 8 * (S - 1), 256:384], 6)
     sent(recv_c.at[0 : S - 1], 2)
-    sent(g_buf.at[0 : SLOT * (M - 1), :], 3)
+    sent(g_buf.at[0 : USED * (M - 1), :], 3)
     sent(gr.at[0 : M - 1], 4)
     sent(rows.at[0 : S - 1], 5)
-    out_f.wait()
-    out_a.wait()
 
 
 def copy_kernel(*refs):
-    n = (len(refs) - 2) // 3
-    ins, outs, held = refs[:n], refs[n : 2 * n], refs[2 * n : 3 * n]
-    in_sem, out_sem = refs[3 * n :]
-    loads = [pltpu.make_async_copy(ins[k], held[k], in_sem.at[k]) for k in range(n)]
-    stores = [pltpu.make_async_copy(held[k], outs[k], out_sem.at[k]) for k in range(n)]
-    for load in loads:
-        load.start()
-    for load, store in zip(loads, stores):
-        load.wait()
+    n = (len(refs) - 1) // 2
+    stores = [pltpu.make_async_copy(refs[k], refs[n + k], refs[-1].at[k]) for k in range(n)]
+    for store in stores:
         store.start()
     for store in stores:
         store.wait()
 
 
 def handed_on(arrays):
-    hbm = pl.BlockSpec(memory_space=pl.ANY)
     n = len(arrays)
+    arrays = [pltpu.with_memory_space_constraint(a, pltpu.VMEM) for a in arrays]
     return pl.pallas_call(
         copy_kernel,
         out_shape=[jax.ShapeDtypeStruct(a.shape, a.dtype) for a in arrays],
-        in_specs=[hbm] * n,
-        out_specs=[hbm] * n,
-        scratch_shapes=[pltpu.VMEM(a.shape, a.dtype) for a in arrays]
-        + [pltpu.SemaphoreType.DMA((n,)), pltpu.SemaphoreType.DMA((n,))],
+        in_specs=[pl.BlockSpec(memory_space=pltpu.VMEM)] * n,
+        out_specs=[pl.BlockSpec(memory_space=pl.ANY)] * n,
+        scratch_shapes=[pltpu.SemaphoreType.DMA((n,))],
         name="hand_on",
     )(*arrays)
 
@@ -477,13 +468,13 @@
     outs = pl.pallas_call(
         functools.partial(kernel, S, M),
         out_shape=(
-            jax.ShapeDtypeStruct((4, N * CH), f32),
-            jax.ShapeDtypeStruct((4, N * CH), f32),
-            jax.ShapeDtypeStruct((3, 4, 12), f32),
-            jax.ShapeDtypeStruct((1, M), f32),
+            pltpu.VMEM((4, N * CH), f32),
+            pltpu.VMEM((4, N * CH), f32),
+            pltpu.VMEM((3, 4, 12), f32),
+            pltpu.VMEM((1, M), f32),
         ),
         in_specs=[hbm] * 7,
-        out_specs=(hbm, hbm, vmem, vmem),
+        out_specs=(vmem,) * 4,
         scratch_shapes=[
             pltpu.VMEM((4 * CH, N), f32),
             pltpu.VMEM((4, N * CH), f32),
@@ -500,15 +491,14 @@
             pltpu.VMEM((4, LANES), f32),
             pltpu.VMEM((M, 4, LANES), f32),
             pltpu.VMEM((N, LANES), f32),
-            pltpu.VMEM((2 * N, LANES), f32),
+            pltpu.VMEM((N, LANES), f32),
             pltpu.VMEM((S, 1, LANES), f32),
             pltpu.VMEM((S, 1, LANES), f32),
             pltpu.VMEM((5, 4, N, LANES), f32),
             pltpu.VMEM((8 * N, LANES), f32),
+            pltpu.VMEM((2, N, 2 * LANES), f32),
             pltpu.VMEM((4 * N, LANES), f32),
             pltpu.VMEM((S // 2, 8, 384), f32),
-            pltpu.VMEM((4, N * CH), f32),
-            pltpu.VMEM((4, N * CH), f32),
             pltpu.VMEM((SLOT * M, LANES), f32),
             pltpu.VMEM((SLOT * M, LANES), f32),
             pltpu.VMEM((M, 1, LANES), f32),
@@ -517,7 +507,6 @@
             pltpu.VMEM((S, 1, LANES), f32),
             pltpu.SemaphoreType.DMA((7,)),
             pltpu.SemaphoreType.DMA((7,)),
-            pltpu.SemaphoreType.DMA((2,)),
             pltpu.SemaphoreType.DMA((7,)),
         ],
         compiler_params=pltpu.CompilerParams(collective_id=0, has_side_effects=True),

time: 72.6 us -> 70.7 us (0.974)
  Pallas kernels: 71.8 us -> 70 us
    pallas_call x1, Pallas kernels: 1.85 us -> 0.85 us  [handed_on(): pl.pallas_call(copy_kernel, out_shape=[jax.ShapeDtypeStruct(a.shape, a.dt...]
    pallas_call x1, Pallas kernels: 70 us -> 69.1 us  [shards(): pl.pallas_call(functools.partial(kernel, S, M), out_shape=(pltpu.VMEM((4,...]
where the time goes in v3:
time: 70.7 us; the launch traced here: 70.6 us
  Pallas kernels  70 us (99%)
    pallas_call x1, Pallas kernels, shards(): pl.pallas_call(functools.partial(kernel, S, M), out_shape=(pltpu.VMEM((4,...  69.1 us

profile of v3, /device:TPU:1, one launch (start us, length us, event | category | flops | bytes accessed | tf_op | source)
XLA Modules:
  0.0 70.6 jit_solution(15543487719130483991)
XLA Ops:
  0.6 69.1 %substep.1 = (f32[4,18432]{1,0:T(4,128)S(1)}, f32[4,18432]{1,0:T(4,128)S(1)}, f32[3,4,12]{2,1,0:T(4,128)S(1)}, f32[1,16]{1,0:T(1,128)S(1)}) custom-call(f32[384,192]{1,0:T(8,128)} %bitcast.5, f32[4,18432]{1,0:T(4,128)} %bitcast.6, f32[3,4,12]{2,1,0:T(4,128)} %v_hbm.1, f32[384,192]{1,0:T(8,128)} %constant.8.clone.a_hbm, f32[192,192]{1,0:T(8,128)} %constant.9.clone.dy_hbm, ...), custom_call_target="tpu_custom_call" | custom-call | tf_op jit(solution)/shard_map/substep/pallas_call | solution.py:468
  69.8 0.9 %hand_on.1 = (f32[4,18432]{1,0:T(4,128)}, f32[4,18432]{1,0:T(4,128)}, f32[3,4,12]{2,1,0:T(4,128)}, f32[1,16]{1,0:T(1,128)}) custom-call(f32[4,18432]{1,0:T(4,128)S(1)} %get-tuple-element.12.refs_0_, f32[4,18432]{1,0:T(4,128)S(1)} %get-tuple-element.13.refs_1_, f32[3,4,12]{2,1,0:T(4,128)S(1)} %get-tuple-element.14.refs_2_, f32[1,16]{1,0:T(1,128)S(1)} %get-tuple-element.15.refs_3_), custom_call_target="tpu_custom_call" | custom-call | tf_op jit(solution)/shard_map/hand_on/pallas_call | solution.py:452

commit v4 on v3

--- a/solution.py
+++ b/solution.py
@@ -21,6 +21,7 @@
 LANES = 128
 SLOT = 40
 USED = 36
+EXPAND = 6
 
 
 def cheb_matrix(points):
@@ -42,6 +43,12 @@
     return np.pi / (points - 1) * np.sin(np.pi * index / (points - 1))
 
 
+def parts_of(matrix):
+    hi = matrix.astype(jnp.bfloat16)
+    mid = (matrix - hi.astype(np.float32)).astype(jnp.bfloat16)
+    return np.stack([hi, mid])
+
+
 def constants(space, members):
     points = 4 * space
     diff = cheb_matrix(points).astype(np.float32)
@@ -53,7 +60,7 @@
     lane_w[:, :9] = np.repeat(root, CH).reshape(members, 9, LANES)
     z_w = np.zeros((space, 8, LANES), np.float32)
     z_w[:, :4] = root.reshape(space, 4, 1)
-    return both, diff, lane_w, z_w
+    return parts_of(both), diff, parts_of(diff), lane_w, z_w
 
 
 def mm(a, b, transpose_b=False):
@@ -69,9 +76,13 @@
     return hi, mid, lo
 
 
+def mm_bf(a, b, contract_b=0):
+    dims = (((1,), (contract_b,)), ((), ()))
+    return lax.dot_general(a, b, dims, preferred_element_type=jnp.float32)
+
+
 def mm_exact(parts, b):
-    dot = lambda a: jnp.dot(a, b, preferred_element_type=jnp.float32)
-    return (dot(parts[2]) + dot(parts[1])) + dot(parts[0])
+    return (mm_bf(parts[2], b) + mm_bf(parts[1], b)) + mm_bf(parts[0], b)
 
 
 def iota(shape, axis):
@@ -86,6 +97,7 @@
     v_hbm,
     a_hbm,
     dy_hbm,
+    dp_hbm,
     wl_hbm,
     wz_hbm,
     f_loc,
@@ -97,6 +109,7 @@
     v_ref,
     a_ref,
     dy_ref,
+    dp_ref,
     wl_ref,
     wz_ref,
     sel_p,
@@ -130,21 +143,27 @@
     m = lax.axis_index("member")
     s = lax.axis_index("space")
 
+    def wrap(value, size):
+        return jnp.where(value >= size, value - size, value)
+
     def over_space(body):
         def step(k, carry):
-            body(lax.rem(s + k, S))
-            body(lax.rem(s + S - k, S))
+            body(wrap(s + k, S))
+            body(wrap(s + S - k, S))
             return carry
 
         lax.fori_loop(1, H, step, 0)
-        body(lax.rem(s + H, S))
+        body(wrap(s + H, S))
+
+    def each_space(body):
+        for k in range(1, H):
+            body(wrap(s + k, S))
+            body(wrap(s + S - k, S))
+        body(wrap(s + H, S))
 
     def over_member(body):
-        def step(k, carry):
-            body(lax.rem(m + k, M))
-            return carry
-
-        lax.fori_loop(1, M, step, 0)
+        for k in range(1, M):
+            body(wrap(m + k, M))
 
     def push(src, dst, which, member, space):
         pltpu.make_async_remote_copy(
@@ -173,6 +192,7 @@
                 (p_hbm, p_ref),
                 (a_hbm, a_ref),
                 (dy_hbm, dy_ref),
+                (dp_hbm, dp_ref),
                 (reg_hbm, reg_ref),
                 (wl_hbm.at[m], wl_ref),
                 (wz_hbm.at[s], wz_ref),
@@ -186,7 +206,7 @@
     over_member(
         lambda t: pl.semaphore_signal(barrier, inc=1, device_id=(t, s), device_id_type=MESH)
     )
-    over_space(
+    each_space(
         lambda t: pl.semaphore_signal(barrier, inc=1, device_id=(m, t), device_id_type=MESH)
     )
 
@@ -202,7 +222,10 @@
     )
     loads[1].wait()
     loads[2].wait()
-    send_b[...] = mm(a_ref[...], p_ref[...], transpose_b=True)
+    q_hi, q_mid, q_lo = split(p_ref[...])
+    send_b[...] = (
+        (mm_bf(a_ref[0], q_lo, 1) + mm_bf(a_ref[1], q_hi, 1)) + mm_bf(a_ref[0], q_mid, 1)
+    ) + mm_bf(a_ref[0], q_hi, 1)
     pl.semaphore_wait(barrier, S - 1 + M - 1)
 
     over_member(lambda t: push(own_x, gath_x.at[m], 0, t, s))
@@ -265,30 +288,35 @@
     keep(send_c.at[s], recv_c.at[s], 2)
     bulk(256, 384, 6)
 
+    lane8 = iota((8, LANES), 1)
+
+    def expand(last):
+        def go(step, carry):
+            for u in range(EXPAND):
+                r = EXPAND * step + u
+                base = pl.ds(pl.multiple_of(8 * r, 8), 8)
+                v1 = recv_b[base, 128:256]
+                if last:
+                    v2 = recv_b[base, 256:384]
+                    tiles = (
+                        jnp.where(lane8 < 64, pltpu.roll(v1, 64, 1), pltpu.roll(v2, 64, 1)),
+                        pltpu.roll(v2, 96, 1),
+                    )
+                else:
+                    v0 = recv_b[base, 0:128]
+                    tiles = (
+                        v0,
+                        jnp.where(lane8 < 32, pltpu.roll(v0, 32, 1), pltpu.roll(v1, 32, 1)),
+                    )
+                for i, v in enumerate(tiles):
+                    at = 32 * r + 8 * (i + 2 * last)
+                    sbuf[pl.ds(pl.multiple_of(at, 8), 8), :] = v
+            return carry
+
+        lax.fori_loop(0, S // EXPAND, go, 0)
+
     arrived(recv_b.at[:, 0:256], 1)
-    arrived(recv_b.at[:, 256:384], 6)
-    lane8 = iota((8, LANES), 1)
-
-    def expand(step, carry):
-        for u in range(3):
-            r = 3 * step + u
-            base = pl.ds(pl.multiple_of(8 * r, 8), 8)
-            v0 = recv_b[base, 0:128]
-            v1 = recv_b[base, 128:256]
-            v2 = recv_b[base, 256:384]
-            y1 = jnp.where(lane8 < 32, pltpu.roll(v0, 32, 1), pltpu.roll(v1, 32, 1))
-            y2 = jnp.where(lane8 < 64, pltpu.roll(v1, 64, 1), pltpu.roll(v2, 64, 1))
-            y3 = pltpu.roll(v2, 96, 1)
-            for i, v in enumerate((v0, y1, y2, y3)):
-                sbuf[pl.ds(pl.multiple_of(32 * r + 8 * i, 8), 8), :] = v
-        return carry
-
-    lax.fori_loop(0, S // 3, expand, 0)
-    for pair in range(2):
-        q2 = jnp.concatenate(
-            [sbuf[pl.ds(2 * pair + i, N, stride=8), :] for i in range(2)], axis=1
-        )
-        dyq_b[pair] = mm(dy_ref[...], q2)
+    expand(0)
 
     arrived(recv_c, 2)
     lane_s = iota((S, LANES), 1) % 4
@@ -303,6 +331,16 @@
         for k in range(4):
             coef[k, z] = spread_p[:, LANES * k : LANES * (k + 1)]
         coef[4, z] = spread_y[:, LANES * z : LANES * (z + 1)]
+
+
+    arrived(recv_b.at[:, 256:384], 6)
+    expand(1)
+    for pair in range(2):
+        q2 = jnp.concatenate(
+            [sbuf[pl.ds(2 * pair + i, N, stride=8), :] for i in range(2)], axis=1
+        )
+        q_hi, q_mid, _ = split(q2)
+        dyq_b[pair] = (mm_bf(dp_ref[0], q_mid) + mm_bf(dp_ref[1], q_hi)) + mm_bf(dp_ref[0], q_hi)
 
     lane_n = iota((N, LANES), 1)
     lorentz = jnp.where(lane_n % 3 == 1, 0.0, lorentz_rate)
@@ -346,7 +384,8 @@
     def slot_of(t):
         return pl.ds(pl.multiple_of(SLOT * t, 8), USED)
 
-    def finish(g, carry):
+    def finish(step, carry):
+        g = lax.rem(m + 1 + step, S // 6)
         for h in range(2):
             slot = h * (S // 6) + g
             base = pl.multiple_of(SLOT * slot, 8)
@@ -423,7 +462,7 @@
     keep(gp.at[m], gr.at[m], 4)
     arrived(gr, 4)
     row[...] = jnp.sum(gr[...], axis=0)
-    over_space(lambda t: push(row, rows.at[s], 5, m, t))
+    each_space(lambda t: push(row, rows.at[s], 5, m, t))
     keep(row, rows.at[s], 5)
     arrived(rows, 5)
     outg_ref[...] = (jnp.sum(rows[...], axis=0) / CH)[:, 0:M]
@@ -462,7 +501,7 @@
 def shards(S, M, perturb, register, ref_velocity):
     N = 4 * S
     f32 = jnp.float32
-    both, diff, lane_w, z_w = constants(S, M)
+    both, diff, diff_parts, lane_w, z_w = constants(S, M)
     vmem = pl.BlockSpec(memory_space=pltpu.VMEM)
     hbm = pl.BlockSpec(memory_space=pl.ANY)
     outs = pl.pallas_call(
@@ -473,14 +512,15 @@
             pltpu.VMEM((3, 4, 12), f32),
             pltpu.VMEM((1, M), f32),
         ),
-        in_specs=[hbm] * 7,
+        in_specs=[hbm] * 8,
         out_specs=(vmem,) * 4,
         scratch_shapes=[
             pltpu.VMEM((4 * CH, N), f32),
             pltpu.VMEM((4, N * CH), f32),
             pltpu.VMEM((3, 4, 12), f32),
-            pltpu.VMEM((2 * N, N), f32),
+            pltpu.VMEM((2, 2 * N, N), jnp.bfloat16),
             pltpu.VMEM((N, N), f32),
+            pltpu.VMEM((2, N, N), jnp.bfloat16),
             pltpu.VMEM((16, LANES), f32),
             pltpu.VMEM((8, LANES), f32),
             pltpu.VMEM((4, LANES, 4 * LANES), jnp.bfloat16),
@@ -507,7 +547,7 @@
             pltpu.VMEM((S, 1, LANES), f32),
             pltpu.SemaphoreType.DMA((7,)),
             pltpu.SemaphoreType.DMA((7,)),
-            pltpu.SemaphoreType.DMA((7,)),
+            pltpu.SemaphoreType.DMA((8,)),
         ],
         compiler_params=pltpu.CompilerParams(collective_id=0, has_side_effects=True),
         name="substep",
@@ -517,6 +557,7 @@
         ref_velocity,
         jnp.asarray(both),
         jnp.asarray(diff),
+        jnp.asarray(diff_parts),
         jnp.asarray(lane_w),
         jnp.asarray(z_w),
     )

time: 70.7 us -> 67.9 us (0.960)
  Pallas kernels: 70 us -> 67.1 us
    pallas_call x1, Pallas kernels: 69.1 us -> 66.3 us  [shards(): pl.pallas_call(functools.partial(kernel, S, M), out_shape=(pltpu.VMEM((4,...]
where the time goes in v4:
time: 67.9 us; the launch traced here: 67.8 us
  Pallas kernels  67.1 us (99%)
    pallas_call x1, Pallas kernels, shards(): pl.pallas_call(functools.partial(kernel, S, M), out_shape=(pltpu.VMEM((4,...  66.3 us

profile of v4, /device:TPU:1, one launch (start us, length us, event | category | flops | bytes accessed | tf_op | source)
XLA Modules:
  0.0 67.8 jit_solution(15407583942685070665)
XLA Ops:
  0.6 66.3 %substep.1 = (f32[4,18432]{1,0:T(4,128)S(1)}, f32[4,18432]{1,0:T(4,128)S(1)}, f32[3,4,12]{2,1,0:T(4,128)S(1)}, f32[1,16]{1,0:T(1,128)S(1)}) custom-call(f32[384,192]{1,0:T(8,128)} %bitcast.5, f32[4,18432]{1,0:T(4,128)} %bitcast.6, f32[3,4,12]{2,1,0:T(4,128)} %v_hbm.1, bf16[2,384,192]{2,1,0:T(8,128)(2,1)} %constant.10.clone.a_hbm, ...), custom_call_target="tpu_custom_call" | custom-call | tf_op jit(solution)/shard_map/substep/pallas_call | solution.py:507
  66.9 0.9 %hand_on.1 = (f32[4,18432]{1,0:T(4,128)}, f32[4,18432]{1,0:T(4,128)}, f32[3,4,12]{2,1,0:T(4,128)}, f32[1,16]{1,0:T(1,128)}) custom-call(f32[4,18432]{1,0:T(4,128)S(1)} %get-tuple-element.12.refs_0_, f32[4,18432]{1,0:T(4,128)S(1)} %get-tuple-element.13.refs_1_, f32[3,4,12]{2,1,0:T(4,128)S(1)} %get-tuple-element.14.refs_2_, f32[1,16]{1,0:T(1,128)S(1)} %get-tuple-element.15.refs_3_), custom_call_target="tpu_custom_call" | custom-call | tf_op jit(solution)/shard_map/hand_on/pallas_call | solution.py:491

commit v5 on v4

--- a/solution.py
+++ b/solution.py
@@ -22,6 +22,7 @@
 SLOT = 40
 USED = 36
 EXPAND = 6
+FAR = {8: (4, 3, 5, 2, 6, 1, 7, 0), 1: (0,)}
 
 
 def cheb_matrix(points):
@@ -82,7 +83,7 @@
 
 
 def mm_exact(parts, b):
-    return (mm_bf(parts[2], b) + mm_bf(parts[1], b)) + mm_bf(parts[0], b)
+    return mm_bf(jnp.concatenate(parts, axis=1), b)
 
 
 def iota(shape, axis):
@@ -127,7 +128,6 @@
     sbuf,
     dyq_b,
     tbuf,
-    rbuf,
     f_buf,
     g_buf,
     gp,
@@ -154,6 +154,29 @@
 
         lax.fori_loop(1, H, step, 0)
         body(wrap(s + H, S))
+
+    def far_space(body):
+        ny = S // 6
+        core = lax.rem(s, 2)
+        y = lax.rem(s // 2, ny)
+        z = s // (2 * ny)
+
+        def step(k, carry):
+            column = wrap(z + lax.rem(k, 3), 3) * ny
+            side = wrap(core + k // 3, 2)
+            for dy in FAR[ny]:
+                t = (column + wrap(y + dy, ny)) * 2 + side
+                if dy == 0:
+
+                    @pl.when(k != 0)
+                    def _():
+                        body(t)
+
+                else:
+                    body(t)
+            return carry
+
+        lax.fori_loop(0, 6, step, 0)
 
     def each_space(body):
         for k in range(1, H):
@@ -244,7 +267,7 @@
                 t,
             )
 
-        over_space(one)
+        far_space(one)
         keep(send_b.at[mine, lanes], recv_b.at[mine, lanes], which)
 
     bulk(0, 256, 1)
@@ -262,10 +285,12 @@
             (group == 12 + 3 * z + comp).astype(jnp.float32),
         ]
         for k in range(4):
-            sel_p[z, :, LANES * k : LANES * (k + 1)] = chosen[k].astype(jnp.bfloat16)
-        sel_d[:, LANES * z : LANES * (z + 1)] = (
-            (group == 3 * z + comp).astype(jnp.float32).astype(jnp.bfloat16)
-        )
+            one = chosen[k].astype(jnp.bfloat16)
+            for i in range(3):
+                sel_p[z, LANES * i : LANES * (i + 1), LANES * k : LANES * (k + 1)] = one
+        one = (group == 3 * z + comp).astype(jnp.float32).astype(jnp.bfloat16)
+        for i in range(3):
+            sel_d[LANES * i : LANES * (i + 1), LANES * z : LANES * (z + 1)] = one
     for load in loads[3:]:
         load.wait()
 
@@ -277,7 +302,11 @@
             xz[12 * k + 4 * j : 12 * k + 4 * j + 4, :] = part
     x = jnp.where(iota((N, LANES), 1) < 12, xz[...], 0.0)
     xz[...] = x
-    ct[...] = mm(dy_ref[...], x)
+    x_hi, x_mid, x_lo = split(x)
+    ct[...] = (
+        (mm_bf(dp_ref[0], x_lo) + mm_bf(dp_ref[1], x_mid))
+        + (mm_bf(dp_ref[0], x_mid) + mm_bf(dp_ref[1], x_hi))
+    ) + mm_bf(dp_ref[0], x_hi)
     packed = xz[pl.ds(0, S, stride=4), :]
     for z in range(1, 4):
         packed = packed + pltpu.roll(xz[pl.ds(z, S, stride=4), :], 12 * z, 1)
@@ -342,41 +371,11 @@
         q_hi, q_mid, _ = split(q2)
         dyq_b[pair] = (mm_bf(dp_ref[0], q_mid) + mm_bf(dp_ref[1], q_hi)) + mm_bf(dp_ref[0], q_hi)
 
-    lane_n = iota((N, LANES), 1)
+    lane_n = iota((24, LANES), 1)
     lorentz = jnp.where(lane_n % 3 == 1, 0.0, lorentz_rate)
-
     real = lane_n % 6 < 3
     comp_n = lane_n % 3
-    half = N // 2
-    for z in range(4):
-        q = sbuf[pl.ds(z, N, stride=8), :]
-        dzq = sbuf[pl.ds(4 + z, N, stride=8), :]
-        dyq = dyq_b[z // 2, :, LANES * (z % 2) : LANES * (z % 2 + 1)]
-        up1 = pltpu.roll(q, LANES - 1, 1)
-        up2 = pltpu.roll(q, LANES - 2, 1)
-        down1 = pltpu.roll(q, 1, 1)
-        qz = jnp.where(comp_n == 0, up2, jnp.where(comp_n == 1, up1, q))
-        qy = jnp.where(comp_n == 0, up1, jnp.where(comp_n == 1, q, down1))
-        other = jnp.where(real, pltpu.roll(q, LANES - 3, 1), pltpu.roll(q, 3, 1))
-        rhs = (-coef[0, z] * dzq - qz * coef[3, z]) + (
-            -coef[1, z] * dyq + coef[2, z] * other - qy * coef[4, z] - lorentz * q
-        )
-        tbuf[pl.ds(z, half, stride=8), :] = rhs[0:half]
-        tbuf[pl.ds(4 + z, half, stride=8), :] = rhs[half:N]
-
-    def compact(step, carry):
-        for u in range(3):
-            r = 3 * step + u
-            t = [tbuf[pl.ds(pl.multiple_of(32 * r + 8 * i, 8), 8), :] for i in range(4)]
-            t1 = pltpu.roll(t[1], 96, 1)
-            t2 = pltpu.roll(t[2], 64, 1)
-            t3 = pltpu.roll(t[3], 32, 1)
-            rbuf[r, :, 0:128] = jnp.where(lane8 < 96, t[0], t1)
-            rbuf[r, :, 128:256] = jnp.where(lane8 < 64, t1, t2)
-            rbuf[r, :, 256:384] = jnp.where(lane8 < 32, t2, t3)
-        return carry
-
-    lax.fori_loop(0, H // 3, compact, 0)
+    lane4 = iota((4, LANES), 1)
     z_rows = 4 * s + iota((4, 384), 0)
     z_mask = (z_rows > 0) & (z_rows < N - 1)
     lane_y = iota((4, 384), 1) // CH
@@ -385,16 +384,51 @@
         return pl.ds(pl.multiple_of(SLOT * t, 8), USED)
 
     def finish(step, carry):
-        g = lax.rem(m + 1 + step, S // 6)
+        if M == 16:
+            off = jnp.where(step < 4, step + 4, jnp.where(step < 6, step - 2, step - 6))
+        else:
+            off = step
+        g = wrap(m // 2 + off, M // 2)
+        at_y = pl.ds(pl.multiple_of(24 * g, 8), 24)
+        for z in range(4):
+            q = sbuf[pl.ds(192 * g + z, 24, stride=8), :]
+            dzq = sbuf[pl.ds(192 * g + 4 + z, 24, stride=8), :]
+            dyq = dyq_b[z // 2, at_y, LANES * (z % 2) : LANES * (z % 2 + 1)]
+            up1 = pltpu.roll(q, LANES - 1, 1)
+            up2 = pltpu.roll(q, LANES - 2, 1)
+            down1 = pltpu.roll(q, 1, 1)
+            qz = jnp.where(comp_n == 0, up2, jnp.where(comp_n == 1, up1, q))
+            qy = jnp.where(comp_n == 0, up1, jnp.where(comp_n == 1, q, down1))
+            other = jnp.where(real, pltpu.roll(q, LANES - 3, 1), pltpu.roll(q, 3, 1))
+            tbuf[pl.ds(z, 24, stride=8), :] = (
+                -coef[0, z, at_y, :] * dzq - qz * coef[3, z, at_y, :]
+            ) + (
+                -coef[1, z, at_y, :] * dyq
+                + coef[2, z, at_y, :] * other
+                - qy * coef[4, z, at_y, :]
+                - lorentz * q
+            )
         for h in range(2):
-            slot = h * (S // 6) + g
+            slot = 2 * g + h
             base = pl.multiple_of(SLOT * slot, 8)
             for i in range(3):
-                r = h * H + 3 * g + i
+                local = 3 * h + i
+                r = 6 * g + local
+                t = [tbuf[32 * local + 8 * k : 32 * local + 8 * k + 4, :] for k in range(4)]
+                t1 = pltpu.roll(t[1], 96, 1)
+                t2 = pltpu.roll(t[2], 64, 1)
+                t3 = pltpu.roll(t[3], 32, 1)
+                rhs = jnp.concatenate(
+                    [
+                        jnp.where(lane4 < 96, t[0], t1),
+                        jnp.where(lane4 < 64, t1, t2),
+                        jnp.where(lane4 < 32, t2, t3),
+                    ],
+                    axis=1,
+                )
                 at = pl.ds(pl.multiple_of(384 * r, 128), 384)
                 y = 4 * r + lane_y
                 mask = jnp.where(z_mask & (y > 0) & (y < N - 1), 1.0, 0.0)
-                rhs = rbuf[3 * g + i, 4 * h : 4 * h + 4, :]
                 q = recv_b[pl.ds(pl.multiple_of(8 * r, 8), 4), :]
                 acc = mask * (alpha_coef * reg_ref[:, at] + time_step * rhs)
                 field = mask * (q + beta_coef * acc)
@@ -409,7 +443,7 @@
 
         return carry
 
-    lax.fori_loop(0, S // 6, finish, 0)
+    lax.fori_loop(0, M // 2, finish, 0)
 
     keep(f_buf.at[slot_of(m), :], g_buf.at[slot_of(m), :], 3)
     pick = (iota((16, N), 1) == 12 * m + iota((16, N), 0)).astype(jnp.float32)
@@ -523,8 +557,8 @@
             pltpu.VMEM((2, N, N), jnp.bfloat16),
             pltpu.VMEM((16, LANES), f32),
             pltpu.VMEM((8, LANES), f32),
-            pltpu.VMEM((4, LANES, 4 * LANES), jnp.bfloat16),
-            pltpu.VMEM((LANES, 4 * LANES), jnp.bfloat16),
+            pltpu.VMEM((4, 3 * LANES, 4 * LANES), jnp.bfloat16),
+            pltpu.VMEM((3 * LANES, 4 * LANES), jnp.bfloat16),
             pltpu.VMEM((2 * N, 384), f32),
             pltpu.VMEM((2 * N, 384), f32),
             pltpu.VMEM((LANES, LANES), f32),
@@ -537,8 +571,7 @@
             pltpu.VMEM((5, 4, N, LANES), f32),
             pltpu.VMEM((8 * N, LANES), f32),
             pltpu.VMEM((2, N, 2 * LANES), f32),
-            pltpu.VMEM((4 * N, LANES), f32),
-            pltpu.VMEM((S // 2, 8, 384), f32),
+            pltpu.VMEM((8 * 24, LANES), f32),
             pltpu.VMEM((SLOT * M, LANES), f32),
             pltpu.VMEM((SLOT * M, LANES), f32),
             pltpu.VMEM((M, 1, LANES), f32),

time: 67.9 us -> 67.6 us (level)
  no operation moved by 1% of the time
where the time goes in v5:
time: 67.6 us; the launch traced here: 67.4 us
  Pallas kernels  66.8 us (99%)
    pallas_call x1, Pallas kernels, shards(): pl.pallas_call(functools.partial(kernel, S, M), out_shape=(pltpu.VMEM((4,...  65.9 us

profile of v5, /device:TPU:1, one launch (start us, length us, event | category | flops | bytes accessed | tf_op | source)
XLA Modules:
  0.0 67.4 jit_solution(13709137641664475608)
XLA Ops:
  0.6 65.9 %substep.1 = (f32[4,18432]{1,0:T(4,128)S(1)}, f32[4,18432]{1,0:T(4,128)S(1)}, f32[3,4,12]{2,1,0:T(4,128)S(1)}, f32[1,16]{1,0:T(1,128)S(1)}) custom-call(f32[384,192]{1,0:T(8,128)} %bitcast.5, f32[4,18432]{1,0:T(4,128)} %bitcast.6, f32[3,4,12]{2,1,0:T(4,128)} %v_hbm.1, bf16[2,384,192]{2,1,0:T(8,128)(2,1)} %constant.10.clone.a_hbm, ...), custom_call_target="tpu_custom_call" | custom-call | tf_op jit(solution)/shard_map/substep/pallas_call | solution.py:541
  66.6 0.9 %hand_on.1 = (f32[4,18432]{1,0:T(4,128)}, f32[4,18432]{1,0:T(4,128)}, f32[3,4,12]{2,1,0:T(4,128)}, f32[1,16]{1,0:T(1,128)}) custom-call(f32[4,18432]{1,0:T(4,128)S(1)} %get-tuple-element.12.refs_0_, f32[4,18432]{1,0:T(4,128)S(1)} %get-tuple-element.13.refs_1_, f32[3,4,12]{2,1,0:T(4,128)S(1)} %get-tuple-element.14.refs_2_, f32[1,16]{1,0:T(1,128)S(1)} %get-tuple-element.15.refs_3_), custom_call_target="tpu_custom_call" | custom-call | tf_op jit(solution)/shard_map/hand_on/pallas_call | solution.py:525

commit v6 on v5

--- a/solution.py
+++ b/solution.py
@@ -474,7 +474,7 @@
             value = tpose[at : at + 1, 0:12]
             outr_ref[c, z : z + 1, :] = time_step * jnp.where(inside, value, 0.0)
 
-    gp[...] = jnp.zeros((M, 1, LANES), jnp.float32)
+    gp[...] = jnp.zeros((2, LANES), jnp.float32)
     arrived(g_buf.at[0 : USED * M, :], 3)
     values = []
     for t in range(9):
@@ -491,23 +491,46 @@
     three = (nine[2 * M : 3 * M] + nine[M : 2 * M]) + nine[0:M]
     part = (three[:, 2 * M : 3 * M] + three[:, M : 2 * M]) + three[:, 0:M]
     for k in range(M):
-        gp[k, :, 0:M] = part[k : k + 1, :]
-    over_member(lambda t: push(gp.at[t], gr.at[m], 4, t, s))
-    keep(gp.at[m], gr.at[m], 4)
+        at, lane = divmod(M * k, LANES)
+        gp[at : at + 1, lane : lane + M] = part[k : k + 1, :]
+    nx, ny = min(4, M), S // 6
+    z_hi, x_at = m // nx, lax.rem(m, nx)
+    z_lo, y_at, core = s // (2 * ny), lax.rem(s // 2, ny), lax.rem(s, 2)
+    mine = (x_at * ny + y_at) * 2 + core
+    column, sides = z_lo * ny, (core, 1 - core)
+    for dy in FAR[ny]:
+        y_to = column + wrap(y_at + dy, ny)
+        for dx in sorted(range(nx), key=lambda d: -min(d, nx - d)):
+            to = z_hi * nx + wrap(x_at + dx, nx)
+            for side in (1, 0):
+                if dy or dx or side:
+                    push(gp, gr.at[mine], 4, to, y_to * 2 + sides[side])
+    keep(gp, gr.at[mine], 4)
     arrived(gr, 4)
     row[...] = jnp.sum(gr[...], axis=0)
-    each_space(lambda t: push(row, rows.at[s], 5, m, t))
-    keep(row, rows.at[s], 5)
+    n_hi = M // nx
+    level = z_hi * 3 + z_lo
+    for dh in sorted(range(n_hi), key=lambda d: -min(d, n_hi - d)):
+        to = wrap(z_hi + dh, n_hi) * nx + x_at
+        for dl in (1, 2, 0):
+            if dh or dl:
+                push(row, rows.at[level], 5, to, (wrap(z_lo + dl, 3) * ny + y_at) * 2 + core)
+    keep(row, rows.at[level], 5)
     arrived(rows, 5)
-    outg_ref[...] = (jnp.sum(rows[...], axis=0) / CH)[:, 0:M]
+    total = jnp.sum(rows[...], axis=0) / CH
+    found = jnp.zeros((1, M), jnp.float32)
+    for k in range(M):
+        at, lane = divmod(M * k, LANES)
+        found = jnp.where(m == k, total[at : at + 1, lane : lane + M], found)
+    outg_ref[...] = found
 
     sent(gath_x.at[0 : M - 1], 0)
     sent(recv_b.at[0 : 8 * (S - 1), 0:256], 1)
     sent(recv_b.at[0 : 8 * (S - 1), 256:384], 6)
     sent(recv_c.at[0 : S - 1], 2)
     sent(g_buf.at[0 : USED * (M - 1), :], 3)
-    sent(gr.at[0 : M - 1], 4)
-    sent(rows.at[0 : S - 1], 5)
+    sent(gr.at[0 : 2 * nx * ny - 1], 4)
+    sent(rows.at[0 : 3 * n_hi - 1], 5)
 
 
 def copy_kernel(*refs):
@@ -574,10 +597,10 @@
             pltpu.VMEM((8 * 24, LANES), f32),
             pltpu.VMEM((SLOT * M, LANES), f32),
             pltpu.VMEM((SLOT * M, LANES), f32),
-            pltpu.VMEM((M, 1, LANES), f32),
-            pltpu.VMEM((M, 1, LANES), f32),
-            pltpu.VMEM((1, LANES), f32),
-            pltpu.VMEM((S, 1, LANES), f32),
+            pltpu.VMEM((2, LANES), f32),
+            pltpu.VMEM((min(4, M) * S // 3, 2, LANES), f32),
+            pltpu.VMEM((2, LANES), f32),
+            pltpu.VMEM((3 * (M // min(4, M)), 2, LANES), f32),
             pltpu.SemaphoreType.DMA((7,)),
             pltpu.SemaphoreType.DMA((7,)),
             pltpu.SemaphoreType.DMA((8,)),

time: 67.6 us -> 67.6 us (level)
  no operation moved by 1% of the time
where the time goes in v6:
time: 67.6 us; the launch traced here: 67.5 us
  Pallas kernels  66.9 us (99%)
    pallas_call x1, Pallas kernels, shards(): pl.pallas_call(functools.partial(kernel, S, M), out_shape=(pltpu.VMEM((4,...  66 us

profile of v6, /device:TPU:1, one launch (start us, length us, event | category | flops | bytes accessed | tf_op | source)
XLA Modules:
  0.0 67.5 jit_solution(16939177230998960902)
XLA Ops:
  0.6 66.0 %substep.1 = (f32[4,18432]{1,0:T(4,128)S(1)}, f32[4,18432]{1,0:T(4,128)S(1)}, f32[3,4,12]{2,1,0:T(4,128)S(1)}, f32[1,16]{1,0:T(1,128)S(1)}) custom-call(f32[384,192]{1,0:T(8,128)} %bitcast.5, f32[4,18432]{1,0:T(4,128)} %bitcast.6, f32[3,4,12]{2,1,0:T(4,128)} %v_hbm.1, bf16[2,384,192]{2,1,0:T(8,128)(2,1)} %constant.10.clone.a_hbm, ...), custom_call_target="tpu_custom_call" | custom-call | tf_op jit(solution)/shard_map/substep/pallas_call | solution.py:564
  66.6 0.9 %hand_on.1 = (f32[4,18432]{1,0:T(4,128)}, f32[4,18432]{1,0:T(4,128)}, f32[3,4,12]{2,1,0:T(4,128)}, f32[1,16]{1,0:T(1,128)}) custom-call(f32[4,18432]{1,0:T(4,128)S(1)} %get-tuple-element.12.refs_0_, f32[4,18432]{1,0:T(4,128)S(1)} %get-tuple-element.13.refs_1_, f32[3,4,12]{2,1,0:T(4,128)S(1)} %get-tuple-element.14.refs_2_, f32[1,16]{1,0:T(1,128)S(1)} %get-tuple-element.15.refs_3_), custom_call_target="tpu_custom_call" | custom-call | tf_op jit(solution)/shard_map/hand_on/pallas_call | solution.py:548

commit v7 on v6

--- a/solution.py
+++ b/solution.py
@@ -61,7 +61,7 @@
     lane_w[:, :9] = np.repeat(root, CH).reshape(members, 9, LANES)
     z_w = np.zeros((space, 8, LANES), np.float32)
     z_w[:, :4] = root.reshape(space, 4, 1)
-    return parts_of(both), diff, parts_of(diff), lane_w, z_w
+    return parts_of(both), parts_of(diff), lane_w, z_w
 
 
 def mm(a, b, transpose_b=False):
@@ -97,7 +97,6 @@
     reg_hbm,
     v_hbm,
     a_hbm,
-    dy_hbm,
     dp_hbm,
     wl_hbm,
     wz_hbm,
@@ -109,7 +108,6 @@
     reg_ref,
     v_ref,
     a_ref,
-    dy_ref,
     dp_ref,
     wl_ref,
     wz_ref,
@@ -179,10 +177,18 @@
         lax.fori_loop(0, 6, step, 0)
 
     def each_space(body):
-        for k in range(1, H):
-            body(wrap(s + k, S))
-            body(wrap(s + S - k, S))
-        body(wrap(s + H, S))
+        ny = S // 6
+        core = lax.rem(s, 2)
+        y = lax.rem(s // 2, ny)
+        z = s // (2 * ny)
+        columns = [wrap(z + dz, 3) * ny for dz in range(3)]
+        sides = [core, 1 - core]
+        for dy in FAR[ny]:
+            at = wrap(y + dy, ny)
+            for dz in (1, 2, 0):
+                for side in (1, 0):
+                    if dy or dz or side:
+                        body((columns[dz] + at) * 2 + sides[side])
 
     def over_member(body):
         for k in range(1, M):
@@ -214,7 +220,6 @@
                 (v_hbm, v_ref),
                 (p_hbm, p_ref),
                 (a_hbm, a_ref),
-                (dy_hbm, dy_ref),
                 (dp_hbm, dp_ref),
                 (reg_hbm, reg_ref),
                 (wl_hbm.at[m], wl_ref),
@@ -226,11 +231,11 @@
         load.start()
 
     barrier = pltpu.get_barrier_semaphore()
+    each_space(
+        lambda t: pl.semaphore_signal(barrier, inc=1, device_id=(m, t), device_id_type=MESH)
+    )
     over_member(
         lambda t: pl.semaphore_signal(barrier, inc=1, device_id=(t, s), device_id_type=MESH)
-    )
-    each_space(
-        lambda t: pl.semaphore_signal(barrier, inc=1, device_id=(m, t), device_id_type=MESH)
     )
 
     tpose[...] = jnp.zeros((LANES, LANES), jnp.float32)
@@ -302,11 +307,14 @@
             xz[12 * k + 4 * j : 12 * k + 4 * j + 4, :] = part
     x = jnp.where(iota((N, LANES), 1) < 12, xz[...], 0.0)
     xz[...] = x
-    x_hi, x_mid, x_lo = split(x)
-    ct[...] = (
-        (mm_bf(dp_ref[0], x_lo) + mm_bf(dp_ref[1], x_mid))
-        + (mm_bf(dp_ref[0], x_mid) + mm_bf(dp_ref[1], x_hi))
-    ) + mm_bf(dp_ref[0], x_hi)
+    def slope(parts):
+        hi, mid, lo = parts
+        return (
+            (mm_bf(dp_ref[0], lo) + mm_bf(dp_ref[1], mid))
+            + (mm_bf(dp_ref[0], mid) + mm_bf(dp_ref[1], hi))
+        ) + mm_bf(dp_ref[0], hi)
+
+    ct[...] = slope(split(x))
     packed = xz[pl.ds(0, S, stride=4), :]
     for z in range(1, 4):
         packed = packed + pltpu.roll(xz[pl.ds(z, S, stride=4), :], 12 * z, 1)
@@ -352,8 +360,8 @@
     for k in range(4):
         xz[pl.ds(k, S, stride=4), :] = jnp.where(lane_s == k, recv_c[:, 0, :], 0.0)
     points = xz[...]
-    dpoints = mm(dy_ref[...], points)
     parts = split(points)
+    dpoints = slope(parts)
     spread_y = mm_exact(split(dpoints), sel_d[...])
     for z in range(4):
         spread_p = mm_exact(parts, sel_p[z])
@@ -558,7 +566,7 @@
 def shards(S, M, perturb, register, ref_velocity):
     N = 4 * S
     f32 = jnp.float32
-    both, diff, diff_parts, lane_w, z_w = constants(S, M)
+    both, diff_parts, lane_w, z_w = constants(S, M)
     vmem = pl.BlockSpec(memory_space=pltpu.VMEM)
     hbm = pl.BlockSpec(memory_space=pl.ANY)
     outs = pl.pallas_call(
@@ -569,14 +577,13 @@
             pltpu.VMEM((3, 4, 12), f32),
             pltpu.VMEM((1, M), f32),
         ),
-        in_specs=[hbm] * 8,
+        in_specs=[hbm] * 7,
         out_specs=(vmem,) * 4,
         scratch_shapes=[
             pltpu.VMEM((4 * CH, N), f32),
             pltpu.VMEM((4, N * CH), f32),
             pltpu.VMEM((3, 4, 12), f32),
             pltpu.VMEM((2, 2 * N, N), jnp.bfloat16),
-            pltpu.VMEM((N, N), f32),
             pltpu.VMEM((2, N, N), jnp.bfloat16),
             pltpu.VMEM((16, LANES), f32),
             pltpu.VMEM((8, LANES), f32),
@@ -603,7 +610,7 @@
             pltpu.VMEM((3 * (M // min(4, M)), 2, LANES), f32),
             pltpu.SemaphoreType.DMA((7,)),
             pltpu.SemaphoreType.DMA((7,)),
-            pltpu.SemaphoreType.DMA((8,)),
+            pltpu.SemaphoreType.DMA((7,)),
         ],
         compiler_params=pltpu.CompilerParams(collective_id=0, has_side_effects=True),
         name="substep",
@@ -612,7 +619,6 @@
         register[0],
         ref_velocity,
         jnp.asarray(both),
-        jnp.asarray(diff),
         jnp.asarray(diff_parts),
         jnp.asarray(lane_w),
         jnp.asarray(z_w),

time: 67.6 us -> 66.9 us (0.990)
  Pallas kernels: 66.9 us -> 66.1 us
    pallas_call x1, Pallas kernels: 66 us -> 65.2 us  [shards(): pl.pallas_call(functools.partial(kernel, S, M), out_shape=(pltpu.VMEM((4,...]
where the time goes in v7:
time: 66.9 us; the launch traced here: 66.7 us
  Pallas kernels  66.1 us (99%)
    pallas_call x1, Pallas kernels, shards(): pl.pallas_call(functools.partial(kernel, S, M), out_shape=(pltpu.VMEM((4,...  65.2 us

profile of v7, /device:TPU:1, one launch (start us, length us, event | category | flops | bytes accessed | tf_op | source)
XLA Modules:
  0.0 66.7 jit_solution(1859694304896125970)
XLA Ops:
  0.6 65.2 %substep.1 = (f32[4,18432]{1,0:T(4,128)S(1)}, f32[4,18432]{1,0:T(4,128)S(1)}, f32[3,4,12]{2,1,0:T(4,128)S(1)}, f32[1,16]{1,0:T(1,128)S(1)}) custom-call(f32[384,192]{1,0:T(8,128)} %bitcast.5, f32[4,18432]{1,0:T(4,128)} %bitcast.6, f32[3,4,12]{2,1,0:T(4,128)} %v_hbm.1, bf16[2,384,192]{2,1,0:T(8,128)(2,1)} %constant.8.clone.a_hbm, ...), custom_call_target="tpu_custom_call" | custom-call | tf_op jit(solution)/shard_map/substep/pallas_call | solution.py:572
  65.9 0.9 %hand_on.1 = (f32[4,18432]{1,0:T(4,128)}, f32[4,18432]{1,0:T(4,128)}, f32[3,4,12]{2,1,0:T(4,128)}, f32[1,16]{1,0:T(1,128)}) custom-call(f32[4,18432]{1,0:T(4,128)S(1)} %get-tuple-element.12.refs_0_, f32[4,18432]{1,0:T(4,128)S(1)} %get-tuple-element.13.refs_1_, f32[3,4,12]{2,1,0:T(4,128)S(1)} %get-tuple-element.14.refs_2_, f32[1,16]{1,0:T(1,128)S(1)} %get-tuple-element.15.refs_3_), custom_call_target="tpu_custom_call" | custom-call | tf_op jit(solution)/shard_map/hand_on/pallas_call | solution.py:556

commit v8 on v7

--- a/solution.py
+++ b/solution.py
@@ -491,13 +491,13 @@
             value = g_buf[pl.ds(4 * t + z, M, stride=SLOT), :]
             values.append(split(value * (weight_y * wz_ref[z : z + 1, :])))
     stack = jnp.concatenate(
-        [jnp.concatenate([v[k] for v in values], axis=1) for k in range(3)], axis=0
+        [jnp.concatenate([v[k] for v in values], axis=1) for k in range(2)], axis=0
     )
-    nine = lax.dot_general(
+    four = lax.dot_general(
         stack, stack, (((1,), (1,)), ((), ())), preferred_element_type=jnp.float32
     )
-    three = (nine[2 * M : 3 * M] + nine[M : 2 * M]) + nine[0:M]
-    part = (three[:, 2 * M : 3 * M] + three[:, M : 2 * M]) + three[:, 0:M]
+    two = four[M : 2 * M] + four[0:M]
+    part = two[:, M : 2 * M] + two[:, 0:M]
     for k in range(M):
         at, lane = divmod(M * k, LANES)
         gp[at : at + 1, lane : lane + M] = part[k : k + 1, :]

time: 66.9 us -> 66.7 us (level)
  no operation moved by 1% of the time
where the time goes in v8:
time: 66.7 us; the launch traced here: 66.6 us
  Pallas kernels  65.9 us (99%)
    pallas_call x1, Pallas kernels, shards(): pl.pallas_call(functools.partial(kernel, S, M), out_shape=(pltpu.VMEM((4,...  65.1 us

profile of v8, /device:TPU:1, one launch (start us, length us, event | category | flops | bytes accessed | tf_op | source)
XLA Modules:
  0.0 66.6 jit_solution(10435302133896264124)
XLA Ops:
  0.6 65.1 %substep.1 = (f32[4,18432]{1,0:T(4,128)S(1)}, f32[4,18432]{1,0:T(4,128)S(1)}, f32[3,4,12]{2,1,0:T(4,128)S(1)}, f32[1,16]{1,0:T(1,128)S(1)}) custom-call(f32[384,192]{1,0:T(8,128)} %bitcast.5, f32[4,18432]{1,0:T(4,128)} %bitcast.6, f32[3,4,12]{2,1,0:T(4,128)} %v_hbm.1, bf16[2,384,192]{2,1,0:T(8,128)(2,1)} %constant.8.clone.a_hbm, ...), custom_call_target="tpu_custom_call" | custom-call | tf_op jit(solution)/shard_map/substep/pallas_call | solution.py:572
  65.7 0.9 %hand_on.1 = (f32[4,18432]{1,0:T(4,128)}, f32[4,18432]{1,0:T(4,128)}, f32[3,4,12]{2,1,0:T(4,128)}, f32[1,16]{1,0:T(1,128)}) custom-call(f32[4,18432]{1,0:T(4,128)S(1)} %get-tuple-element.12.refs_0_, f32[4,18432]{1,0:T(4,128)S(1)} %get-tuple-element.13.refs_1_, f32[3,4,12]{2,1,0:T(4,128)S(1)} %get-tuple-element.14.refs_2_, f32[1,16]{1,0:T(1,128)S(1)} %get-tuple-element.15.refs_3_), custom_call_target="tpu_custom_call" | custom-call | tf_op jit(solution)/shard_map/hand_on/pallas_call | solution.py:556
